TPU v7x, 32 devices: a whole 2x2x4 slice. The times are simulated.
32 devices in a mesh: dp: 8 (over z, x), tensor: 4 (over y, core).
Axes of the slice: x: 2, y: 2, z: 4, core: 2. Of those that a mesh axis runs over, the one named last changes fastest.
Arguments:
- block_in: bfloat16 [16384, 1024], P(('dp', 'tensor')), may hold values from -6 to 6
- segments: int32 [16, 1024], P('dp'), may hold values from 0 to 4, as said below
- first_gain: float32 [1024], replicated, may hold values from 0.5 to 1.5
- first_shift: float32 [1024], replicated, may hold values from -1.25 to 1.25
- w_qkv: bfloat16 [1024, 3, 1024], P(None, None, 'tensor'), may hold values from -0.1875 to 0.1875
- qv_bias: float32 [2, 1024], P(None, 'tensor'), may hold values from -1.75 to 1.75
- w_mix: bfloat16 [1024, 1024], P('tensor'), may hold values from -0.75 to 0.75
- mix_bias: float32 [1024], replicated, may hold values from -1.25 to 1.25
- second_gain: float32 [1024], replicated, may hold values from 0.5 to 1.5
- second_shift: float32 [1024], replicated, may hold values from -1.25 to 1.25
- w_expand: bfloat16 [1024, 4096], P(None, 'tensor'), may hold values from -0.1875 to 0.1875
- expand_bias: float32 [4096], P('tensor'), may hold values from -1.75 to 1.75
- w_reduce: bfloat16 [4096, 1024], P('tensor'), may hold values from -0.125 to 0.125
- reduce_bias: float32 [1024], replicated, may hold values from -1.25 to 1.25
- out_grad: bfloat16 [16384, 1024], P(('dp', 'tensor')), may hold values from -6 to 6
Outputs:
- block_out: bfloat16 [16384, 1024], P(('dp', 'tensor'))
- in_grad: float32 [16384, 1024], P(('dp', 'tensor'))
- first_gain_grad: float32 [1024], replicated
- first_shift_grad: float32 [1024], replicated
- qkv_grad: float32 [1024, 3, 1024], P(None, None, 'tensor')
- qv_bias_grad: float32 [2, 1024], P(None, 'tensor')
- mix_grad: float32 [1024, 1024], P('tensor')
- mix_bias_grad: float32 [1024], replicated
- second_gain_grad: float32 [1024], replicated
- second_shift_grad: float32 [1024], replicated
- expand_grad: float32 [1024, 4096], P(None, 'tensor')
- expand_bias_grad: float32 [4096], P('tensor')
- reduce_grad: float32 [4096, 1024], P('tensor')
- reduce_bias_grad: float32 [1024], replicated
Inputs may be any that keep to these rules, and one draw needn't show every extreme that they name: `segments`: each row of 1024 tokens holds five documents numbered 0 to 4 in order, each a run of consecutive tokens; document 2 starts before token 256 and its last token is at position 768 or later.
All inputs are finite; a program needn't handle non-finite values.
Results may differ from a plain program's by a relative error of at most 0.014.
Values may be sent and summed in bfloat16 or wider, within the bound.
A program may use at most 192 MiB of HBM per device.

v0:
```python
import functools

import jax
import jax.numpy as jnp
from jax import lax
from jax.experimental import pallas as pl
from jax.experimental.pallas import tpu as pltpu
from jax.sharding import PartitionSpec as P

HD = 64
PAIR = 2 * HD
QB = 256
EPS = 1e-5
BF = jnp.bfloat16
F32 = jnp.float32
SCALE = HD ** (-0.5)
MESH_ID = pl.DeviceIdType.MESH
EARLY = 1
AHEAD = 4
NT = (((1,), (1,)), ((), ()))
TN = (((0,), (0,)), ((), ()))


def dot(a, b, dims=(((1,), (0,)), ((), ()))):
    return lax.dot_general(a, b, dims, preferred_element_type=F32)


def norm_stats(values):
    mean = jnp.mean(values, axis=-1, keepdims=True)
    centered = values - mean
    variance = jnp.mean(centered * centered, axis=-1, keepdims=True)
    scale = lax.rsqrt(variance + EPS)
    return centered * scale, scale


def fill_bias(seg_ref, row, bias_ref, blocks):
    segr = seg_ref[pl.ds(row, 1), :].astype(F32)
    segc = jnp.broadcast_to(segr, (8, segr.shape[1])).T[:, 0:1]
    off = 0
    for i in range(blocks):
        keys = (i + 1) * QB
        kpos = lax.broadcasted_iota(jnp.int32, (keys, QB), 0)
        qpos = lax.broadcasted_iota(jnp.int32, (keys, QB), 1) + i * QB
        same = segc[:keys, :] == segr[:, i * QB : (i + 1) * QB]
        allowed = jnp.logical_and(kpos <= qpos, same)
        bias_ref[off : off + keys, :] = jnp.where(allowed, 0.0, -1e30)
        off += keys


def half_masks():
    lane = lax.broadcasted_iota(jnp.int32, (1, PAIR), 1)
    return (lane < HD, lane >= HD)


def ring_index(at, n):
    at = (at + 2 * n) % n
    far = at // (n // 2)
    return (1 - far) * 2 * at + far * (2 * (n - 1 - at) + 1)


def ring_place(n):
    mine = lax.axis_index("dp")
    odd = mine % 2
    pos = (1 - odd) * (mine // 2) + odd * (n - 1 - mine // 2)
    return mine, pos, (ring_index(pos + 1, n), ring_index(pos - 1, n))


def meet(tensor_peers, dp_peers):
    barrier = pltpu.get_barrier_semaphore()
    for other in tensor_peers:
        pl.semaphore_signal(barrier, inc=1, device_id={"tensor": other}, device_id_type=MESH_ID)
    for other in dp_peers:
        pl.semaphore_signal(barrier, inc=1, device_id={"dp": other}, device_id_type=MESH_ID)
    pl.semaphore_wait(barrier, len(tensor_peers) + len(dp_peers))


def both_heads(a, masks):
    zero = jnp.zeros_like(a)
    return jnp.concatenate([jnp.where(masks[0], a, zero), jnp.where(masks[1], a, zero)], axis=0)


def twice(a):
    return jnp.concatenate([a, a], axis=1)


def fwd_kernel(
    n,
    x_ref, seg_ref, g1_ref, s1_ref, bq_ref, mixb_ref, g2_ref, s2_ref, wq_hbm, wm_hbm, og_ref,
    rows1_out, qkv_out, att_out, resid_out, n2_out, wqf_out, wmf_out, oga_ref,
    rows1_ref, qkv_ref, att_ref, resid_ref, n2_ref, w_all, wm_all,
    b_all, bqf, bias_ref, psend, pgot, send, recv, ring_send, ring_recv, local, out,
):
    rows, width = x_ref.shape
    seq = rows1_ref.shape[0]
    cols = w_all.shape[3]
    wqf_ref = w_all.at[1]
    wmf_ref = wm_all.at[1]
    cols3 = 3 * cols
    half = rows // 2
    blocks = seq // QB
    me = lax.axis_index("tensor")
    core = me % 2
    sib = me + 1 - 2 * core
    far = (me + 2) % 4
    mine, pos, sides = ring_place(n)
    meet((sib, far), sides)

    def remote(src, dst, k, other):
        return pltpu.make_async_remote_copy(
            src_ref=src,
            dst_ref=dst,
            send_sem=send.at[k],
            recv_sem=recv.at[k],
            device_id={"tensor": other},
            device_id_type=MESH_ID,
        )

    slab = width // n
    wide = cols // 2

    def slab_rows(chunk):
        return pl.ds(pl.multiple_of(chunk * slab, slab), slab)

    def piece():
        return remote(wq_hbm.at[:, slab_rows(mine)], wqf_ref.at[:, slab_rows(mine)], 0, far)

    def bias_across():
        return remote(bq_ref, bqf, 1, far)

    def own_half(c):
        return pl.ds(pl.multiple_of(core * rows + c * half, half), half)

    def rows_beside(c):
        return remote(rows1_ref.at[own_half(c)], rows1_ref.at[own_half(c)], 2 + c, sib)

    def mix_across():
        return remote(wm_hbm, wmf_ref, 4, far)

    def og_across(c):
        return remote(
            og_ref.at[pl.ds(c * half, half)], oga_ref.at[pl.ds((2 + c) * rows, half)], 5 + c, far
        )

    def og_beside():
        return remote(og_ref, oga_ref.at[pl.ds(rows, rows)], 7, sib)

    def og_forward(c):
        return remote(
            oga_ref.at[pl.ds((2 + c) * rows, half)],
            oga_ref.at[pl.ds((2 + c) * rows + half, half)],
            8 + c,
            sib,
        )

    def part_beside():
        return remote(psend, pgot, 10, sib)

    def og_own():
        return pltpu.make_async_copy(og_ref, oga_ref.at[pl.ds(0, rows)], local.at[0])

    def hop(k, d, s):
        chunk = ring_index(pos - s if d == 0 else pos + s, n)
        ref = wqf_ref.at[k, slab_rows(chunk), d * wide : (d + 1) * wide]
        return pltpu.make_async_remote_copy(
            src_ref=ref,
            dst_ref=ref,
            send_sem=ring_send.at[k, d],
            recv_sem=ring_recv.at[k, d, s],
            device_id={"dp": sides[d]},
            device_id_type=MESH_ID,
        )

    def tick(s):
        for k in range(3):
            for d in range(2):
                hop(k, d, s).wait()

                @pl.when(s < n - 2)
                def _():
                    hop(k, d, s + 1).start()

    def put(k):
        near = pl.ds(0, cols3)
        far_part = pl.ds(cols3, cols3)
        low, high = pl.ds(0, half), pl.ds(half, half)
        src, dst = (
            (rows1_ref, rows1_out),
            (qkv_ref.at[:, near], qkv_out.at[:, near]),
            (qkv_ref.at[:, far_part], qkv_out.at[:, far_part]),
            (wqf_ref, wqf_out),
            (wmf_ref, wmf_out),
            (att_ref, att_out),
            (resid_ref.at[low], resid_out.at[low]),
            (resid_ref.at[high], resid_out.at[high]),
            (n2_ref.at[low], n2_out.at[low]),
            (n2_ref.at[high], n2_out.at[high]),
        )[k]
        return pltpu.make_async_copy(src, dst, out.at[k])

    piece().start()
    bias_across().start()
    loads = (
        pltpu.make_async_copy(wq_hbm, w_all.at[0], local.at[1]),
        pltpu.make_async_copy(wm_hbm, wm_all.at[0], local.at[2]),
    )
    for load in loads:
        load.start()
    step = 64
    for c in range(2):

        @pl.loop(0, half // step)
        def _(r):
            normed = norm_stats(x_ref[pl.ds(pl.multiple_of(c * half + r * step, step), step), :].astype(F32))[0]
            to = pl.ds(pl.multiple_of(core * rows + c * half + r * step, step), step)
            rows1_ref[to, :] = (normed * g1_ref[...] + s1_ref[...]).astype(BF)

        rows_beside(c).start()
    piece().wait()
    for k in range(3):
        for d in range(2):
            hop(k, d, 0).start()
    mix_across().start()
    for c in range(2):
        og_across(c).start()
    og_beside().start()
    og_own().start()
    fill_bias(seg_ref, me // 2, bias_ref, blocks)

    def fill_shift(g, ref):
        b_all[g, 0:1] = ref[0:1]
        b_all[g, 1:2] = jnp.zeros_like(ref[0:1])
        b_all[g, 2:3] = ref[1:2]

    fill_shift(0, bq_ref)
    for c in range(2):
        rows_beside(c).wait()
    for load in loads:
        load.wait()
    put(0).start()
    masks = half_masks()
    pairs = cols // PAIR
    ticks = 1 + 2 * pairs

    @pl.loop(0, 2 * pairs)
    def _(p):
        group = p // pairs

        @pl.when(p == pairs)
        def _():
            @pl.loop(ticks, n - 1)
            def _(s):
                tick(s)

            bias_across().wait()
            fill_shift(1, bqf)
            put(3).start()

        @pl.when(p % pairs == 0)
        def _():
            @pl.loop(0, 3)
            def _(k):
                to = pl.ds(pl.multiple_of(group * cols3 + k * cols, cols), cols)
                part = dot(rows1_ref[...], w_all[group, k]) + b_all[group, pl.ds(k, 1)]
                qkv_ref[:, to] = part.astype(BF)

        @pl.when(p == 0)
        def _():
            put(1).start()
            tick(0)

        @pl.when(p == pairs)
        def _():
            put(2).start()

        base = group * cols3 + (p % pairs) * PAIR

        def lanes(k):
            return pl.ds(pl.multiple_of(base + k * cols, PAIR), PAIR)

        vt = qkv_ref[:, lanes(2)].T
        off = 0
        for i in range(blocks):
            keys = (i + 1) * QB
            at = slice(i * QB, (i + 1) * QB)
            qi = qkv_ref[at, lanes(0)] * jnp.asarray(SCALE, BF)
            kk = qkv_ref[:keys, lanes(1)]
            s = dot(kk, both_heads(qi, masks), NT) + twice(bias_ref[off : off + keys, :])
            e = jnp.exp(s - jnp.max(s, axis=0, keepdims=True))
            inverse = 1.0 / jnp.sum(e, axis=0, keepdims=True)
            e = e.astype(BF)
            outs = []
            for h in range(2):
                side = slice(h * QB, (h + 1) * QB)
                outs.append(dot(vt[h * HD : (h + 1) * HD, :keys], e[:, side]) * inverse[:, side])
            att_ref[at, pl.ds(pl.multiple_of(p * PAIR, PAIR), PAIR)] = jnp.concatenate(outs, axis=0).T.astype(BF)
            off += keys
            if i % 2 == 1:

                @pl.when(p < pairs)
                def _():
                    tick(1 + 2 * p + i // 2)

    mix_across().wait()
    put(4).start()
    put(5).start()
    nb = 256

    def mixed(start, at):
        sel = pl.ds(pl.multiple_of(start, rows), rows)
        total = dot(att_ref[sel, 0:cols], wm_all[0, :, at])
        return total + dot(att_ref[sel, cols : 2 * cols], wm_all[1, :, at])

    @pl.loop(0, width // nb)
    def _(k):
        at = pl.ds(pl.multiple_of(k * nb, nb), nb)
        psend[:, at] = mixed((1 - core) * rows, at).astype(BF)

    part_beside().start()

    @pl.loop(0, width // nb)
    def _(k):
        at = pl.ds(pl.multiple_of(k * nb, nb), nb)
        resid_ref[:, at] = x_ref[:, at].astype(F32) + mixed(core * rows, at) + mixb_ref[:, at]

    for c in range(2):
        og_across(c).wait()
        og_forward(c).start()
    part_beside().wait()

    for c in range(2):

        @pl.loop(0, half // step)
        def _(r):
            at = pl.ds(pl.multiple_of(c * half + r * step, step), step)
            full = resid_ref[at, :] + pgot[at, :].astype(F32)
            resid_ref[at, :] = full
            n2_ref[at, :] = (norm_stats(full)[0] * g2_ref[...] + s2_ref[...]).astype(BF)

        put(6 + c).start()
        put(8 + c).start()

    for k in range(10):
        put(k).wait()
    og_own().wait()
    og_beside().wait()
    for c in range(2):
        og_forward(c).wait()


def forward(x, segments, g1, s1, bq, mixb, g2, s2, wq, wm, og, n):
    rows, width = x.shape
    seq = segments.shape[1]
    cols = wq.shape[2]
    blocks = seq // QB
    vmem = pl.BlockSpec(memory_space=pltpu.VMEM)
    anyspace = pl.BlockSpec(memory_space=pl.ANY)
    return pl.pallas_call(
        functools.partial(fwd_kernel, n),
        in_specs=[vmem] * 8 + [anyspace] * 3,
        out_specs=[anyspace] * 8,
        out_shape=[
            jax.ShapeDtypeStruct((seq, width), BF),
            jax.ShapeDtypeStruct((seq, 6 * cols), BF),
            jax.ShapeDtypeStruct((seq, 2 * cols), BF),
            jax.ShapeDtypeStruct((rows, width), F32),
            jax.ShapeDtypeStruct((rows, width), BF),
            jax.ShapeDtypeStruct(wq.shape, BF),
            jax.ShapeDtypeStruct(wm.shape, BF),
            jax.ShapeDtypeStruct((4 * rows, width), BF),
        ],
        scratch_shapes=[
            pltpu.VMEM((seq, width), BF),
            pltpu.VMEM((seq, 6 * cols), BF),
            pltpu.VMEM((seq, 2 * cols), BF),
            pltpu.VMEM((rows, width), F32),
            pltpu.VMEM((rows, width), BF),
            pltpu.VMEM((2,) + wq.shape, BF),
            pltpu.VMEM((2,) + wm.shape, BF),
            pltpu.VMEM((2, 3, cols), F32),
            pltpu.VMEM((2, cols), F32),
            pltpu.VMEM((QB * blocks * (blocks + 1) // 2, QB), F32),
            pltpu.VMEM((rows, width), BF),
            pltpu.VMEM((rows, width), BF),
            pltpu.SemaphoreType.DMA((11,)),
            pltpu.SemaphoreType.DMA((11,)),
            pltpu.SemaphoreType.DMA((3, 2)),
            pltpu.SemaphoreType.DMA((3, 2, n - 1)),
            pltpu.SemaphoreType.DMA((3,)),
            pltpu.SemaphoreType.DMA((10,)),
        ],
        compiler_params=pltpu.CompilerParams(
            collective_id=3, has_side_effects=True, vmem_limit_bytes=56 << 20
        ),
        name="forward",
    )(x, segments, g1, s1, bq, mixb, g2, s2, wq, wm, og)


def bwd_kernel(
    n,
    mg_hbm, qkv_hbm, att_hbm, rows1_hbm, wq_hbm, wqf_hbm, wm_hbm, wmf_hbm, x_hbm, rgrad_hbm, rg_hbm, eg_hbm, carry_hbm,
    seg_ref, g1_ref,
    in_out, qg_out, qsum_ref, nsum_ref, ro_ref, eo_ref,
    in_ref, qg_ref,
    mg, qkv, att, rows1, wq, wqf, wm, wmf, x, rgrad, ffg,
    rbuf, dqkv, ag, bias_ref, dk_ref, dv_ref, q_send, q_got, m_send, m_got, s_got, s_send, psend, pgot, n1g,
    send, recv, ring_send, ring_recv, gather_send, gather_recv, local, out,
):
    rows, width = in_ref.shape
    seq = mg.shape[0]
    cols = wq.shape[2]
    cols3 = 3 * cols
    pairs = cols // PAIR
    blocks = seq // QB
    me = lax.axis_index("tensor")
    core = me % 2
    sib = me + 1 - 2 * core
    far = (me + 2) % 4
    mine, pos, sides = ring_place(n)

    pairs_in = (
        (mg_hbm, mg), (wmf_hbm, wmf), (att_hbm, att), (qkv_hbm, qkv), (rg_hbm, ffg.at[0]), (eg_hbm, ffg.at[1]),
        (rows1_hbm, rows1), (wm_hbm, wm), (wqf_hbm, wqf), (wq_hbm, wq), (x_hbm, x), (rgrad_hbm, rgrad),
    )

    def load(k):
        return pltpu.make_async_copy(pairs_in[k][0], pairs_in[k][1], local.at[k])

    for k in range(len(pairs_in)):
        load(k).start()
    meet((sib, far), sides)

    def remote(src, dst, k, other):
        return pltpu.make_async_remote_copy(
            src_ref=src,
            dst_ref=dst,
            send_sem=send.at[k],
            recv_sem=recv.at[k],
            device_id={"tensor": other},
            device_id_type=MESH_ID,
        )

    def q_across(k):
        return remote(q_send.at[k], q_got.at[k], k, far)

    def m_across():
        return remote(m_send, m_got, 3, far)

    def s_across():
        return remote(s_send, s_got, 4, far)

    def part_beside():
        return remote(psend, pgot, 5, sib)

    def ring_copy(src, kind, d, s):
        return pltpu.make_async_remote_copy(
            src_ref=src,
            dst_ref=rbuf.at[s, kind, d],
            send_sem=ring_send.at[kind, d],
            recv_sem=ring_recv.at[kind, d, s],
            device_id={"dp": sides[d]},
            device_id_type=MESH_ID,
        )

    def part(d, s):
        return ring_index(pos - 1 - s if d == 0 else pos + 1 + s, n)

    def tick(kind, s):
        for d in range(2):
            ring_copy(rbuf.at[s, kind, d], kind, d, s).wait()
            mixed = rbuf[s, kind, d].astype(F32) + ffg[kind, part(d, s + 1), d].astype(F32)
            rbuf[s, kind, d] = mixed.astype(BF)

            @pl.when(s < n - 2)
            def _():
                ring_copy(rbuf.at[s, kind, d], kind, d, s + 1).start()

    outs_hbm = (ro_ref, eo_ref)

    def put(k):
        if isinstance(k, int) and k == 4:
            return pltpu.make_async_copy(in_ref, in_out, out.at[4])
        return pltpu.make_async_copy(qg_ref.at[k], qg_out.at[k], out.at[k])

    def gather(kind, d, s):
        chunk = ring_index(pos - s if d == 0 else pos + s, n)
        ref = outs_hbm[kind].at[chunk, d]
        return pltpu.make_async_remote_copy(
            src_ref=ref,
            dst_ref=ref,
            send_sem=gather_send.at[kind, d],
            recv_sem=gather_recv.at[kind, d, s],
            device_id={"dp": sides[d]},
            device_id_type=MESH_ID,
        )

    def gather_tick(kind, s):
        for d in range(2):
            gather(kind, d, s).wait()

            @pl.when(s + 1 < AHEAD)
            def _():
                gather(kind, d, s + 1).start()

    def gather_begin():
        owns = [
            pltpu.make_async_copy(rbuf.at[n - 2, kind], outs_hbm[kind].at[mine], local.at[12 + kind])
            for kind in range(2)
        ]
        for item in owns:
            item.start()
        for kind in range(2):
            owns[kind].wait()
            for d in range(2):
                gather(kind, d, 0).start()

    for kind in range(2):
        for d in range(2):
            ring_copy(carry_hbm.at[kind, d], kind, d, EARLY).start()

    fill_bias(seg_ref, me // 2, bias_ref, blocks)
    masks = half_masks()
    for k in range(6):
        load(k).wait()
    m_send[...] = dot(mg[...], att[:, cols : 2 * cols], TN).astype(BF)
    m_across().start()
    ag[...] = dot(mg[...], wmf[...], NT).astype(BF)

    turns = 2 * pairs * blocks
    reduce_turns = 2 * (n - 1 - EARLY)
    inside = reduce_turns < turns
    hops = [(h % 2, h // 2) for h in range(max(turns - reduce_turns - 1, 0), 2 * AHEAD)]
    if not inside:
        hops = [(h % 2, h // 2) for h in range(2 * AHEAD)]

    def next_hop():
        if hops:
            gather_tick(*hops.pop(0))

    @pl.loop(0, 2 * pairs)
    def _(q):
        first = q < pairs
        group = 1 - q // pairs
        slot = q % pairs
        base = group * cols3 + slot * PAIR

        @pl.when(q == pairs)
        def _():
            ag[...] = dot(mg[...], wm[...], NT).astype(BF)

        def lanes(k):
            return pl.ds(pl.multiple_of(base + k * cols, PAIR), PAIR)

        own = pl.ds(pl.multiple_of(slot * PAIR, PAIR), PAIR)
        kt = qkv[:, lanes(1)].T
        dk_ref[...] = jnp.zeros_like(dk_ref)
        dv_ref[...] = jnp.zeros_like(dv_ref)
        off = 0
        qsum = jnp.zeros((1, PAIR), F32)
        for i in range(blocks):
            keys = (i + 1) * QB
            at = slice(i * QB, (i + 1) * QB)
            qi = qkv[at, lanes(0)] * jnp.asarray(SCALE, BF)
            gi = ag[at, own]
            kk = qkv[:keys, lanes(1)]
            vv = qkv[:keys, lanes(2)]
            q2 = both_heads(qi, masks)
            g2 = both_heads(gi, masks)
            s = dot(kk, q2, NT) + twice(bias_ref[off : off + keys, :])
            e = jnp.exp(s - jnp.max(s, axis=0, keepdims=True))
            prob = e * (1.0 / jnp.sum(e, axis=0, keepdims=True))
            weighted = prob * dot(vv, g2, NT)
            ds = (weighted - prob * jnp.sum(weighted, axis=0, keepdims=True)).astype(BF)
            dv_ref[:keys, :] += dot(prob.astype(BF), g2)
            dk_ref[:keys, :] += dot(ds, q2)
            outs = []
            for h in range(2):
                outs.append(dot(kt[h * HD : (h + 1) * HD, :keys], ds[:, h * QB : (h + 1) * QB]))
            dq = (jnp.concatenate(outs, axis=0).T * SCALE).astype(BF)
            dqkv[at, lanes(0)] = dq
            qsum += jnp.sum(dq.astype(F32), axis=0, keepdims=True)
            off += keys
            turn = blocks * q + i

            @pl.when(turn < reduce_turns)
            def _():
                tick(i % 2, EARLY + turn // 2)

            if inside and i == reduce_turns % blocks:

                @pl.when(turn == reduce_turns)
                def _():
                    gather_begin()

            if inside:
                hop = turn - reduce_turns - 1

                @pl.when(jnp.logical_and(hop >= 0, hop < 2 * AHEAD))
                def _():
                    gather_tick((i + 1) % 2, hop // 2)
        dv = dv_ref[...].astype(BF)
        dqkv[:, lanes(1)] = dk_ref[...].astype(BF)
        dqkv[:, lanes(2)] = dv
        vsum = jnp.sum(dv.astype(F32), axis=0, keepdims=True)
        for (name, sel) in ((s_send, first), (qsum_ref, jnp.logical_not(first))):

            @pl.when(sel)
            def _():
                name[0:1, own] = qsum
                name[1:2, own] = vsum

        @pl.when(q == pairs - 1)
        def _():
            s_across().start()
            load(6).wait()
            load(7).wait()

            @pl.loop(0, 3)
            def _(k):
                to = pl.ds(pl.multiple_of(cols3 + k * cols, cols), cols)
                q_send[k] = dot(rows1[...], dqkv[:, to], TN).astype(BF)
                q_across(k).start()

    @pl.loop(EARLY + blocks * pairs, n - 1)
    def _(s):
        for kind in range(2):
            tick(kind, s)

    if not inside:
        gather_begin()
    for k in (8, 9):
        load(k).wait()
    nb = 256

    def back(start, at):
        sel = pl.ds(pl.multiple_of(start, rows), rows)
        total = dot(dqkv[sel, 0:cols], wq[0, at, :], NT)
        for k in range(1, 6):
            w = wq if k < 3 else wqf
            total += dot(dqkv[sel, k * cols : (k + 1) * cols], w[k % 3, at, :], NT)
        return total

    @pl.loop(0, width // nb)
    def _(k):
        at = pl.ds(pl.multiple_of(k * nb, nb), nb)
        psend[:, at] = back((1 - core) * rows, at).astype(BF)

    part_beside().start()
    next_hop()

    @pl.loop(0, width // nb)
    def _(k):
        at = pl.ds(pl.multiple_of(k * nb, nb), nb)
        n1g[:, at] = back(core * rows, at)

    next_hop()
    part_beside().wait()
    load(10).wait()
    load(11).wait()
    nsum_ref[...] = jnp.zeros_like(nsum_ref)
    step = 64

    @pl.loop(0, rows // step)
    def _(r):
        at = pl.ds(pl.multiple_of(r * step, step), step)
        grad = n1g[at, :] + pgot[at, :].astype(F32)
        normed, scale = norm_stats(x[at, :].astype(F32))
        g = grad * g1_ref[...]
        mean_g = jnp.mean(g, axis=-1, keepdims=True)
        mean_gn = jnp.mean(g * normed, axis=-1, keepdims=True)
        in_ref[at, :] = rgrad[at, :] + scale * (g - mean_g - normed * mean_gn)
        nsum_ref[0:1, :] += jnp.sum(grad * normed, axis=0, keepdims=True)
        nsum_ref[1:2, :] += jnp.sum(grad, axis=0, keepdims=True)

    put(4).start()
    next_hop()
    mixed = dot(mg[...], att[:, 0:cols], TN)
    m_across().wait()
    qg_ref[3] = (mixed + m_got[...].astype(F32)).astype(BF)
    put(3).start()
    s_across().wait()
    qsum_ref[...] += s_got[...]
    next_hop()

    @pl.loop(0, 3)
    def _(k):
        to = pl.ds(pl.multiple_of(k * cols, cols), cols)
        qg = dot(rows1[...], dqkv[:, to], TN)
        q_across(k).wait()
        qg_ref[k] = (qg + q_got[k].astype(F32)).astype(BF)
        put(k).start()

    while hops:
        next_hop()
    for k in range(5):
        put(k).wait()


def backward(mg, qkv, att, rows1, wq, wqf, wm, wmf, x, rgrad, rg, eg, carry, segments, g1, n):
    rows, width = x.shape
    seq = mg.shape[0]
    cols = wq.shape[2]
    blocks = seq // QB
    vmem = pl.BlockSpec(memory_space=pltpu.VMEM)
    anyspace = pl.BlockSpec(memory_space=pl.ANY)
    split = rg.shape
    chunk = split[2:]
    return pl.pallas_call(
        functools.partial(bwd_kernel, n),
        in_specs=[anyspace] * 13 + [vmem] * 2,
        out_specs=[anyspace] * 2 + [vmem] * 2 + [anyspace] * 2,
        out_shape=[
            jax.ShapeDtypeStruct((rows, width), F32),
            jax.ShapeDtypeStruct((4, width, cols), BF),
            jax.ShapeDtypeStruct((2, cols), F32),
            jax.ShapeDtypeStruct((2, width), F32),
            jax.ShapeDtypeStruct(split, BF),
            jax.ShapeDtypeStruct(split, BF),
        ],
        scratch_shapes=[
            pltpu.VMEM((rows, width), F32),
            pltpu.VMEM((4, width, cols), BF),
            pltpu.VMEM(mg.shape, BF),
            pltpu.VMEM(qkv.shape, BF),
            pltpu.VMEM(att.shape, BF),
            pltpu.VMEM(rows1.shape, BF),
            pltpu.VMEM(wq.shape, BF),
            pltpu.VMEM(wq.shape, BF),
            pltpu.VMEM(wm.shape, BF),
            pltpu.VMEM(wm.shape, BF),
            pltpu.VMEM(x.shape, BF),
            pltpu.VMEM(rgrad.shape, F32),
            pltpu.VMEM((2,) + split, BF),
            pltpu.VMEM((n - 1, 2, 2) + chunk, BF),
            pltpu.VMEM(qkv.shape, BF),
            pltpu.VMEM((seq, cols), BF),
            pltpu.VMEM((QB * blocks * (blocks + 1) // 2, QB), F32),
            pltpu.VMEM((seq, PAIR), F32),
            pltpu.VMEM((seq, PAIR), F32),
            pltpu.VMEM((3, width, cols), BF),
            pltpu.VMEM((3, width, cols), BF),
            pltpu.VMEM((width, cols), BF),
            pltpu.VMEM((width, cols), BF),
            pltpu.VMEM((2, cols), F32),
            pltpu.VMEM((2, cols), F32),
            pltpu.VMEM((rows, width), BF),
            pltpu.VMEM((rows, width), BF),
            pltpu.VMEM((rows, width), F32),
            pltpu.SemaphoreType.DMA((6,)),
            pltpu.SemaphoreType.DMA((6,)),
            pltpu.SemaphoreType.DMA((2, 2)),
            pltpu.SemaphoreType.DMA((2, 2, n - 1)),
            pltpu.SemaphoreType.DMA((2, 2)),
            pltpu.SemaphoreType.DMA((2, 2, n - 1)),
            pltpu.SemaphoreType.DMA((14,)),
            pltpu.SemaphoreType.DMA((5,)),
        ],
        compiler_params=pltpu.CompilerParams(
            collective_id=4, has_side_effects=True, vmem_limit_bytes=60 << 20
        ),
        name="backward",
    )(mg, qkv, att, rows1, wq, wqf, wm, wmf, x, rgrad, rg, eg, carry, segments, g1)


GA = 0.7978845608028654
GB = 0.044715


def ff_kernel(
    n,
    n2_ref, og_hbm, we_hbm, wr_hbm, resid_hbm, be_ref, gain_ref,
    rgrad_out, mg_out, rg_out, eg_out, brn_out, brf_out, usum_ref, dsum_ref, carry_ref,
    rgrad_ref, mg_ref, rg_ref, eg_ref, brn_ref, brf_ref,
    og_ref, we_ref, wr_ref, resid_ref, n2b, act, pg, ng, br, ng_d, br_d, ng_s, br_s, ng_far, ng_out,
    rbuf, send, recv, ring_send, ring_recv, local, out,
):
    rows, width = n2_ref.shape
    units = we_ref.shape[1]
    part = rows // 2
    nb = 256
    me = lax.axis_index("tensor")
    core = me % 2
    sib = me + 1 - 2 * core
    far = (me + 2) % 4

    mine, pos, sides = ring_place(n)
    meet((sib, far), sides)
    h = rg_ref.shape[2]

    def remote(src, dst, k, other):
        return pltpu.make_async_remote_copy(
            src_ref=src,
            dst_ref=dst,
            send_sem=send.at[k],
            recv_sem=recv.at[k],
            device_id={"tensor": other},
            device_id_type=MESH_ID,
        )

    def y_at(c):
        return pl.ds((2 + c) * rows, part)

    def d_at(c):
        return pl.ds((2 + c) * rows + part, part)

    def rows_across(c):
        return remote(n2_ref.at[pl.ds(c * part, part)], n2b.at[y_at(c)], c, far)

    def rows_beside():
        return remote(n2_ref, n2b.at[pl.ds(rows, rows)], 2, sib)

    def rows_forward(c):
        return remote(n2b.at[y_at(c)], n2b.at[d_at(c)], 3 + c, sib)

    def ng_beside():
        return remote(ng.at[pl.ds(rows, rows)], ng_s, 5, sib)

    def br_beside():
        return remote(br.at[pl.ds(rows, rows)], br_s, 6, sib)

    def ng_combine(c):
        return remote(ng.at[d_at(c)], ng_d.at[c], 7 + c, sib)

    def br_combine(c):
        return remote(br.at[d_at(c)], br_d.at[c], 9 + c, sib)

    def ng_across(c):
        return remote(ng_out.at[c], ng_far.at[c], 11 + c, far)

    def own_half(c):
        return pl.ds(pl.multiple_of(core * rows + c * part, part), part)

    def mg_beside(c):
        return remote(mg_ref.at[pl.ds(c * part, part)], mg_out.at[own_half(c)], 13 + c, sib)

    def put(k):
        low, high = pl.ds(0, part), pl.ds(part, part)
        src, dst = (
            (rg_ref, rg_out),
            (eg_ref, eg_out),
            (brn_ref, brn_out),
            (brf_ref, brf_out),
            (rgrad_ref.at[low], rgrad_out.at[low]),
            (rgrad_ref.at[high], rgrad_out.at[high]),
            (mg_ref.at[low], mg_out.at[own_half(0)]),
            (mg_ref.at[high], mg_out.at[own_half(1)]),
        )[k]
        return pltpu.make_async_copy(src, dst, out.at[k])

    for c in range(2):
        rows_across(c).start()
    rows_beside().start()
    first = pl.ds(0, rows)
    rest = pl.ds(rows, 3 * rows)
    loads = [
        pltpu.make_async_copy(n2_ref, n2b.at[first], local.at[0]),
        pltpu.make_async_copy(we_hbm, we_ref, local.at[1]),
        pltpu.make_async_copy(og_hbm.at[first], og_ref.at[first], local.at[2]),
        pltpu.make_async_copy(wr_hbm, wr_ref, local.at[3]),
        pltpu.make_async_copy(og_hbm.at[rest], og_ref.at[rest], local.at[4]),
        pltpu.make_async_copy(resid_hbm, resid_ref, local.at[5]),
    ]
    for load in loads:
        load.start()
    usum_ref[...] = jnp.zeros_like(usum_ref)
    for load in loads[:4]:
        load.wait()

    @pl.loop(0, 4)
    def _(b):
        at = pl.ds(pl.multiple_of(b * rows, rows), rows)
        c = b - 2

        @pl.when(b == 1)
        def _():
            rows_beside().wait()
            loads[4].wait()

        @pl.when(b >= 2)
        def _():
            rows_across(c).wait()
            rows_forward(c).start()
            rows_forward(c).wait()

        for k in range(units // nb):
            cols = slice(k * nb, (k + 1) * nb)
            u = dot(n2b[at, :], we_ref[:, cols]) + be_ref[:, cols]
            act_grad = dot(og_ref[at, :], wr_ref[cols, :], NT)
            sq = u * u
            th = jnp.tanh(u * (GA + (GA * GB) * sq))
            cdf = 0.5 * (1.0 + th)
            slope = cdf + (0.5 * u) * (1.0 - th * th) * (GA + (3.0 * GA * GB) * sq)
            pre = (act_grad * slope).astype(BF)
            act[at, cols] = (u * cdf).astype(BF)
            pg[at, cols] = pre
            usum_ref[:, cols] += jnp.sum(pre.astype(F32), axis=0, keepdims=True)
        @pl.loop(0, width // nb)
        def _(k):
            cols = pl.ds(pl.multiple_of(k * nb, nb), nb)
            ng[at, cols] = dot(pg[at, :], we_ref[cols, :], NT).astype(BF)

        @pl.when(b == 1)
        def _():
            ng_beside().start()

        @pl.when(b >= 2)
        def _():
            ng_combine(c).start()

        @pl.loop(0, width // nb)
        def _(k):
            cols = pl.ds(pl.multiple_of(k * nb, nb), nb)
            br[at, cols] = dot(act[at, :], wr_ref[:, cols]).astype(BF)

        @pl.when(b == 1)
        def _():
            br_beside().start()

        @pl.when(b >= 2)
        def _():
            br_combine(c).start()
            ng_combine(c).wait()
            ng_out[c] = (ng[y_at(c), :].astype(F32) + ng_d[c].astype(F32)).astype(BF)
            ng_across(c).start()

    def part_of(d, s):
        return ring_index(pos - 1 - s if d == 0 else pos + 1 + s, n)

    def ring_copy(src, kind, d, s):
        return pltpu.make_async_remote_copy(
            src_ref=src,
            dst_ref=rbuf.at[s, kind, d],
            send_sem=ring_send.at[kind, d],
            recv_sem=ring_recv.at[kind, d, s],
            device_id={"dp": sides[d]},
            device_id_type=MESH_ID,
        )

    ffg = (rg_ref, eg_ref)

    def ring_start(kind):
        for d in range(2):
            ring_copy(ffg[kind].at[part_of(d, 0), d], kind, d, 0).start()

    def tick(kind, s):
        for d in range(2):
            ring_copy(rbuf.at[s, kind, d], kind, d, s).wait()
            total = rbuf[s, kind, d].astype(F32) + ffg[kind][part_of(d, s + 1), d].astype(F32)
            rbuf[s, kind, d] = total.astype(BF)
            if s + 1 < EARLY:
                ring_copy(rbuf.at[s, kind, d], kind, d, s + 1).start()

    @pl.loop(0, width // nb)
    def _(k):
        cols = pl.ds(pl.multiple_of(k * nb, nb), nb)
        grad = dot(act[...], og_ref[:, cols], TN).astype(BF)
        rg_ref[:, :, :, cols] = grad.reshape(n, 2, h, nb)

    ring_start(0)
    put(0).start()

    @pl.loop(0, width // nb)
    def _(k):
        cols = pl.ds(pl.multiple_of(k * nb, nb), nb)
        grad = dot(n2b[...], pg[:, cols], TN).astype(BF)
        eg_ref[:, :, :, cols] = grad.reshape(n, 2, h, nb)

    ring_start(1)
    put(1).start()
    br_beside().wait()
    brn_ref[...] = (br[0:rows, :].astype(F32) + br_s[...].astype(F32)).astype(BF)
    for c in range(2):
        br_combine(c).wait()
        brf_ref[c * part : (c + 1) * part, :] = (
            br[y_at(c), :].astype(F32) + br_d[c].astype(F32)
        ).astype(BF)
    put(2).start()
    put(3).start()
    ng_beside().wait()
    loads[5].wait()
    dsum_ref[...] = jnp.zeros_like(dsum_ref)
    step = 64
    for c in range(2):
        ng_across(c).wait()

        @pl.loop(0, part // step)
        def _(r):
            inner = pl.ds(pl.multiple_of(r * step, step), step)
            at = pl.ds(pl.multiple_of(c * part + r * step, step), step)
            grad = ng[at, :].astype(F32) + ng_s[at, :].astype(F32) + ng_far[c, inner, :].astype(F32)
            normed, scale = norm_stats(resid_ref[at, :])
            g = grad * gain_ref[...]
            gn = g * normed
            mean_g = jnp.mean(g, axis=-1, keepdims=True)
            mean_gn = jnp.mean(gn, axis=-1, keepdims=True)
            og = og_ref[at, :].astype(F32)
            rgrad = og + scale * (g - mean_g - normed * mean_gn)
            rgrad_ref[at, :] = rgrad
            mg = rgrad.astype(BF)
            mg_ref[at, :] = mg
            dsum_ref[0:1, :] += jnp.sum(mg.astype(F32), axis=0, keepdims=True)
            dsum_ref[1:2, :] += jnp.sum(grad * normed, axis=0, keepdims=True)
            dsum_ref[2:3, :] += jnp.sum(grad, axis=0, keepdims=True)
            dsum_ref[3:4, :] += jnp.sum(og, axis=0, keepdims=True)

        mg_beside(c).start()
        put(4 + c).start()
        put(6 + c).start()
        if c == 0:
            for s in range(EARLY):
                tick(0, s)
    for s in range(EARLY):
        tick(1, s)
    carry_ref[...] = rbuf[EARLY - 1]
    for c in range(2):
        mg_beside(c).wait()
    for k in range(8):
        put(k).wait()


def ff(n2, og_all, we, wr, be, resid, gain, n):
    rows, width = n2.shape
    units = we.shape[1]
    part = rows // 2
    vmem = pl.BlockSpec(memory_space=pltpu.VMEM)
    anyspace = pl.BlockSpec(memory_space=pl.ANY)
    return pl.pallas_call(
        functools.partial(ff_kernel, n),
        in_specs=[anyspace] * 5 + [vmem] * 2,
        out_specs=[anyspace] * 6 + [vmem] * 3,
        out_shape=[
            jax.ShapeDtypeStruct((rows, width), F32),
            jax.ShapeDtypeStruct((2 * rows, width), BF),
            jax.ShapeDtypeStruct((n, 2, units // (2 * n), width), BF),
            jax.ShapeDtypeStruct((n, 2, width // (2 * n), units), BF),
            jax.ShapeDtypeStruct((rows, width), BF),
            jax.ShapeDtypeStruct((rows, width), BF),
            jax.ShapeDtypeStruct((1, units), F32),
            jax.ShapeDtypeStruct((4, width), F32),
            jax.ShapeDtypeStruct((2, 2, units // (2 * n), width), BF),
        ],
        scratch_shapes=[
            pltpu.VMEM((rows, width), F32),
            pltpu.VMEM((rows, width), BF),
            pltpu.VMEM((n, 2, units // (2 * n), width), BF),
            pltpu.VMEM((n, 2, width // (2 * n), units), BF),
            pltpu.VMEM((rows, width), BF),
            pltpu.VMEM((rows, width), BF),
            pltpu.VMEM((4 * rows, width), BF),
            pltpu.VMEM(we.shape, BF),
            pltpu.VMEM(wr.shape, BF),
            pltpu.VMEM((rows, width), F32),
            pltpu.VMEM((4 * rows, width), BF),
            pltpu.VMEM((4 * rows, units), BF),
            pltpu.VMEM((4 * rows, units), BF),
            pltpu.VMEM((4 * rows, width), BF),
            pltpu.VMEM((4 * rows, width), BF),
            pltpu.VMEM((2, part, width), BF),
            pltpu.VMEM((2, part, width), BF),
            pltpu.VMEM((rows, width), BF),
            pltpu.VMEM((rows, width), BF),
            pltpu.VMEM((2, part, width), BF),
            pltpu.VMEM((2, part, width), BF),
            pltpu.VMEM((EARLY, 2, 2, units // (2 * n), width), BF),
            pltpu.SemaphoreType.DMA((15,)),
            pltpu.SemaphoreType.DMA((15,)),
            pltpu.SemaphoreType.DMA((2, 2)),
            pltpu.SemaphoreType.DMA((2, 2, EARLY)),
            pltpu.SemaphoreType.DMA((6,)),
            pltpu.SemaphoreType.DMA((8,)),
        ],
        compiler_params=pltpu.CompilerParams(
            collective_id=2, has_side_effects=True, vmem_limit_bytes=60 << 20
        ),
        name="ff",
    )(n2, og_all, we, wr, resid, be, gain)


def ring_kernel(
    n, g_ref, small_ref, rbias_ref, resid_hbm, brn_hbm, brf_hbm, _r, _e,
    qo_ref, mo_ref, ro_ref, eo_ref, so_ref, bo_ref,
    buf, sbuf, sall, speer, ssum, resid, brn, bro,
    send, recv, fsend, frecv, ssend, srecv, tsend, trecv, local,
):
    mine, pos, sides = ring_place(n)
    me = lax.axis_index("tensor")
    far = (me + 2) % 4
    peers = [(me + k) % 4 for k in range(1, 4)]
    loads = (
        pltpu.make_async_copy(resid_hbm, resid, local.at[0]),
        pltpu.make_async_copy(brn_hbm, brn, local.at[1]),
    )
    for load in loads:
        load.start()
    meet(peers, sides)

    def remote(src, dst, kind, d, s):
        return pltpu.make_async_remote_copy(
            src_ref=src,
            dst_ref=dst,
            send_sem=send.at[kind, d],
            recv_sem=recv.at[kind, d, s],
            device_id={"dp": sides[d]},
            device_id_type=MESH_ID,
        )

    def little(src, dst, kind, s):
        return pltpu.make_async_remote_copy(
            src_ref=src,
            dst_ref=dst,
            send_sem=ssend.at[kind],
            recv_sem=srecv.at[kind, s],
            device_id={"dp": sides[0]},
            device_id_type=MESH_ID,
        )

    def beside(src, dst, k, other):
        return pltpu.make_async_remote_copy(
            src_ref=src,
            dst_ref=dst,
            send_sem=tsend.at[k],
            recv_sem=trecv.at[k],
            device_id={"tensor": other},
            device_id_type=MESH_ID,
        )

    def share(k):
        return beside(small_ref, speer.at[k], k, peers[k])

    def branch():
        return beside(brf_hbm, bro, 3, far)

    def part(d, s):
        return ring_index(pos - 1 - s if d == 0 else pos + 1 + s, n)

    def held(d, s):
        return ring_index(pos - s if d == 0 else pos + s, n)

    streams = [(k, d) for k in range(4) for d in range(2)]

    def source(k, chunk, d):
        return g_ref.at[k, chunk, d]

    def slot(k, s, d):
        return buf.at[s, d, k]

    def put_at(k, chunk, d):
        return qo_ref.at[k, chunk, d] if k < 3 else mo_ref.at[chunk, d]

    def add(k, d, s):
        ref = slot(k, s, d)
        total = ref[...].astype(F32) + source(k, part(d, s + 1), d)[...].astype(F32)
        ref[...] = total.astype(BF)

    def gather(k, d, s):
        ref = put_at(k, held(d, s), d)
        return remote(ref, ref, 4 + k, d, s)

    left = n - 1 - AHEAD
    half = ro_ref.shape[3] // 2

    def ff_hop(kind, c, d, s):
        ref = (ro_ref, eo_ref)[kind].at[held(d, s), d, :, pl.ds(c * half, half)]
        k = 2 * kind + c
        return pltpu.make_async_remote_copy(
            src_ref=ref,
            dst_ref=ref,
            send_sem=fsend.at[k, d],
            recv_sem=frecv.at[k, d, s - AHEAD],
            device_id={"dp": sides[d]},
            device_id_type=MESH_ID,
        )

    def beside_step(kind, s, act):
        @pl.when(s < left)
        def _():
            for d in range(2):
                act(ff_hop(kind, 0, d, AHEAD + s))

        @pl.when(s >= n - 1 - left)
        def _():
            for d in range(2):
                act(ff_hop(kind, 1, d, AHEAD + s - (n - 1 - left)))

    def start(copy):
        copy.start()

    def finish(copy):
        copy.wait()

    def gather_small(s):
        ref = sall.at[held(0, s)]
        return little(ref, ref, 1, s)

    for k, d in streams:
        remote(source(k, part(d, 0), d), slot(k, 0, d), k, d, 0).start()
    for k in range(3):
        share(k).start()
    branch().start()
    for k in range(3):
        share(k).wait()
    ssum[...] = small_ref[...]
    shared = n * 6 // 8
    ssum[0:shared] = ssum[0:shared] + speer[0, 0:shared] + speer[1, 0:shared] + speer[2, 0:shared]
    little(ssum.at[part(0, 0)], sbuf.at[0], 0, 0).start()

    @pl.loop(0, n - 2)
    def _(s):
        beside_step(0, s, start)
        for k, d in streams:
            remote(slot(k, s, d), slot(k, s, d), k, d, s).wait()
            add(k, d, s)
            remote(slot(k, s, d), slot(k, s + 1, d), k, d, s + 1).start()
        little(sbuf.at[s], sbuf.at[s], 0, s).wait()
        sbuf[s] = sbuf[s] + ssum[part(0, s + 1)]
        little(sbuf.at[s], sbuf.at[s + 1], 0, s + 1).start()
        beside_step(0, s, finish)

    last = n - 2
    beside_step(0, last, start)
    puts = []
    for k, d in streams:
        remote(slot(k, last, d), slot(k, last, d), k, d, last).wait()
        add(k, d, last)
        put = pltpu.make_async_copy(slot(k, last, d), put_at(k, mine, d), local.at[2 + 2 * k + d])
        put.start()
        puts.append(put)
    for (k, d), put in zip(streams, puts):
        put.wait()
        gather(k, d, 0).start()
    little(sbuf.at[last], sbuf.at[last], 0, last).wait()
    sall[mine] = sbuf[last] + ssum[mine]
    gather_small(0).start()
    beside_step(0, last, finish)

    @pl.loop(0, n - 2)
    def _(s):
        beside_step(1, s, start)
        for k, d in streams:
            gather(k, d, s).wait()
            gather(k, d, s + 1).start()
        gather_small(s).wait()
        gather_small(s + 1).start()
        beside_step(1, s, finish)

    beside_step(1, last, start)

    branch().wait()
    for load in loads:
        load.wait()
    step = 64

    @pl.loop(0, bo_ref.shape[0] // step)
    def _(r):
        at = pl.ds(pl.multiple_of(r * step, step), step)
        total = resid[at, :] + brn[at, :].astype(F32) + bro[at, :].astype(F32) + rbias_ref[...]
        bo_ref[at, :] = total.astype(BF)

    for k, d in streams:
        gather(k, d, last).wait()
    gather_small(last).wait()
    so_ref[...] = sall[...]
    beside_step(1, last, finish)


def ring_sum(g, small, resid, brn, brf, r, e, rbias, n):
    split = (4, n, 2, g.shape[1] // (2 * n), g.shape[2])
    s3 = small.reshape(n, 1, small.size // n)
    vmem = pl.BlockSpec(memory_space=pltpu.VMEM)
    anyspace = pl.BlockSpec(memory_space=pl.ANY)
    qo, mo, ro, eo, so, bo = pl.pallas_call(
        functools.partial(ring_kernel, n),
        in_specs=[vmem] * 3 + [anyspace] * 5,
        out_specs=[anyspace] * 4 + [vmem] * 2,
        input_output_aliases={6: 2, 7: 3},
        out_shape=[
            jax.ShapeDtypeStruct((3,) + split[1:], BF),
            jax.ShapeDtypeStruct(split[1:], BF),
            jax.ShapeDtypeStruct(r.shape, BF),
            jax.ShapeDtypeStruct(e.shape, BF),
            jax.ShapeDtypeStruct(s3.shape, F32),
            jax.ShapeDtypeStruct(brf.shape, BF),
        ],
        scratch_shapes=[
            pltpu.VMEM((n - 1, 2, 4) + split[3:], BF),
            pltpu.VMEM((n - 1,) + s3.shape[1:], F32),
            pltpu.VMEM(s3.shape, F32),
            pltpu.VMEM((3,) + s3.shape, F32),
            pltpu.VMEM(s3.shape, F32),
            pltpu.VMEM(resid.shape, F32),
            pltpu.VMEM(brn.shape, BF),
            pltpu.VMEM(brf.shape, BF),
            pltpu.SemaphoreType.DMA((8, 2)),
            pltpu.SemaphoreType.DMA((8, 2, n - 1)),
            pltpu.SemaphoreType.DMA((4, 2)),
            pltpu.SemaphoreType.DMA((4, 2, n - 1 - AHEAD)),
            pltpu.SemaphoreType.DMA((2,)),
            pltpu.SemaphoreType.DMA((2, n - 1)),
            pltpu.SemaphoreType.DMA((4,)),
            pltpu.SemaphoreType.DMA((4,)),
            pltpu.SemaphoreType.DMA((10,)),
        ],
        compiler_params=pltpu.CompilerParams(
            collective_id=1, has_side_effects=True, vmem_limit_bytes=60 << 20
        ),
        name="ring_sum",
    )(g.reshape(split), s3, rbias, resid, brn, brf, r, e)
    wide = (-1, r.shape[-1])
    return (
        qo.reshape((3,) + g.shape[1:]),
        mo.reshape(g.shape[1:]),
        ro.reshape(wide),
        eo.reshape(wide),
        so.reshape(small.shape),
        bo,
    )


def body(
    block_in,
    segments,
    first_gain,
    first_shift,
    w_qkv,
    qv_bias,
    w_mix,
    mix_bias,
    second_gain,
    second_shift,
    w_expand,
    expand_bias,
    w_reduce,
    reduce_bias,
    out_grad,
):
    width = block_in.shape[1]
    cols = w_qkv.shape[2]
    units = w_expand.shape[1]
    dp_size = lax.axis_size("dp")
    flat = (1, width)
    wq = w_qkv.transpose(1, 0, 2)
    rows1, qkv, att, resid, n2, wq_far, wm_far, og_all = forward(
        block_in,
        segments,
        first_gain.reshape(flat),
        first_shift.reshape(flat),
        qv_bias,
        mix_bias.reshape(flat),
        second_gain.reshape(flat),
        second_shift.reshape(flat),
        wq,
        w_mix,
        out_grad,
        dp_size,
    )
    resid_grad, mg_all, reduce_grad, expand_grad, br_near, br_far, unit_sums, sums2, carry = ff(
        n2, og_all, w_expand, w_reduce, expand_bias.reshape(1, units), resid, second_gain.reshape(flat), dp_size
    )
    in_grad, grads, qv_sums, norm_sums, reduce_all, expand_all = backward(
        mg_all,
        qkv,
        att,
        rows1,
        wq,
        wq_far,
        w_mix,
        wm_far,
        block_in,
        resid_grad,
        reduce_grad,
        expand_grad,
        carry,
        segments,
        first_gain.reshape(flat),
        dp_size,
    )
    small = jnp.concatenate(
        [
            norm_sums,
            sums2,
            unit_sums,
            jnp.pad(qv_sums.reshape(1, 2 * cols), ((0, 0), (0, width - 2 * cols))),
        ],
        axis=0,
    )
    qkv_grad, mix_grad, reduce_all, expand_all, small, block_out = ring_sum(
        grads,
        small,
        resid,
        br_near,
        br_far,
        reduce_all,
        expand_all,
        reduce_bias.reshape(flat),
        dp_size,
    )
    return (
        block_out,
        in_grad,
        small[0],
        small[1],
        qkv_grad.astype(F32).transpose(1, 0, 2),
        small[7, : 2 * cols].reshape(2, cols),
        mix_grad.astype(F32).T,
        small[2],
        small[3],
        small[4],
        expand_all.astype(F32),
        small[6],
        reduce_all.astype(F32),
        small[5],
    )


def solution(mesh):
    both = P(("dp", "tensor"), None)
    return jax.shard_map(
        body,
        mesh=mesh,
        in_specs=(
            both,
            P("dp", None),
            P(),
            P(),
            P(None, None, "tensor"),
            P(None, "tensor"),
            P("tensor", None),
            P(),
            P(),
            P(),
            P(None, "tensor"),
            P("tensor"),
            P("tensor", None),
            P(),
            both,
        ),
        out_specs=(
            both,
            both,
            P(),
            P(),
            P(None, None, "tensor"),
            P(None, "tensor"),
            P("tensor", None),
            P(),
            P(),
            P(),
            P(None, "tensor"),
            P("tensor"),
            P("tensor", None),
            P(),
        ),
        check_vma=False,
    )
```

profile of v0, /device:TPU:0, one launch (start us, length us, event | category | flops | bytes accessed | tf_op | source)
XLA Modules:
  0.0 264.1 jit_solution(6338240569440791530)
XLA Ops:
  0.6 49.6 %forward.1 = (bf16[1024,1024]{1,0:T(8,128)(2,1)}, bf16[1024,1536]{1,0:T(8,128)(2,1)}, bf16[1024,512]{1,0:T(8,128)(2,1)}, f32[512,1024]{1,0:T(8,128)}, bf16[512,1...) custom-call(bf16[512,1024]{1,0:T(8,128)(2,1)} %x_hbm.1, ...), custom_call_target="tpu_custom_call" | custom-call | tf_op jit(solution)/shard_map/forward/pallas_call | solution.py:357
  50.2 58.2 %ff.1 = (f32[512,1024]{1,0:T(8,128)}, bf16[1024,1024]{1,0:T(8,128)(2,1)}, bf16[8,2,64,1024]{3,2,1,0:T(8,128)(2,1)}, bf16[8,2,64,1024]{3,2,1,0:T(8,128)(2,1)}, bf...) custom-call(bf16[512,1024]{1,0:T(8,128)(2,1)} %get-tuple-element.43., ...), custom_call_target="tpu_custom_call" | custom-call | tf_op jit(solution)/shard_map/ff/pallas_call | solution.py:1026
  108.4 0.0 copy-start.5
  108.4 0.0 copy-start.6
  108.4 69.2 %backward.1 = (f32[512,1024]{1,0:T(8,128)}, bf16[4,1024,256]{2,1,0:T(8,128)(2,1)}, f32[2,256]{1,0:T(2,128)}, f32[2,1024]{1,0:T(2,128)}, bf16[8,2,64,1024]{3,2,1,...) custom-call(bf16[1024,1024]{1,0:T(8,128)(2,1)} %get-tuple-element.46.mg_hbm, bf16[1024,1536]{1,0:T(8,128)(2,1)} %get-tuple-element.47.qkv_hbm, ...), custom_call_target="tpu_custom_call" | custom-call | tf_op jit(solution)/shard_map/backward/pallas_call | solution.py:707
  177.6 0.7 copy.33
  178.3 0.0 copy-done.5
  178.3 0.0 copy-done.6
  178.3 0.7 select_maximum_fusion
  179.0 0.6 reshape.97.small_ref
  179.6 67.9 %ring_sum.1 = (bf16[3,8,2,64,256]{4,3,2,1,0:T(8,128)(2,1)}, bf16[8,2,64,256]{3,2,1,0:T(8,128)(2,1)}, bf16[8,2,64,1024]{3,2,1,0:T(8,128)(2,1)}, bf16[8,2,64,1024]...) custom-call(bf16[4,8,2,64,256]{4,3,2,1,0:T(8,128)(2,1)} %bitcast.39,, ...), custom_call_target="tpu_custom_call", output_to_operand_aliasing={{2}: (6, {}), {3}: (7, {})} | custom-call | tf_op jit(solution)/shard_map/ring_sum/pallas_call | solution.py:1270
  247.5 0.0 copy-start.3
  247.5 1.4 fusion
  249.0 0.8 copy.35
  249.7 0.6 reshape_squeeze.3
  250.3 1.1 bitcast_convert_fusion.2
  251.5 1.3 copy.31
  252.8 0.0 copy-done.3
  252.8 0.0 copy-start
  252.8 0.0 copy-start.1
  252.8 2.0 convert_bitcast_fusion
  254.8 0.1 copy-done
  255.0 1.2 copy-done.1
  256.1 0.0 copy-start.4
  256.1 4.7 %bitcast_convert_fusion = (f32[1024,1024]{1,0:T(8,128)}, f32[1024,1024]{1,0:T(8,128)}) fusion(bf16[8,2,64,1024]{3,2,1,0:T(8,128)(2,1)S(1)} %copy-done, bf16[8,2,64,1024]{3,2,1,0:T(8,128)(2,1)S(1)} %copy-done.1), kind=kLoop, calls=%fused_computation.1 | loop fusion | flops 2097152 | bytes 12582912 | tf_op jit(solution)/shard_map/convert_element_type | solution.py:1409
  260.8 0.0 copy-start.2
  260.9 0.0 copy-done.4
  260.9 1.0 copy.40
  261.8 1.0 copy-done.2
  262.8 1.3 copy.41
  (1 shorter events, 0.0 us)
Async XLA Ops:
  108.4 69.9 %copy-start.5 = (f32[4,1024]{1,0:T(4,128)S(1)}, f32[4,1024]{1,0:T(4,128)}, u32[]{:S(2)}) copy-start(f32[4,1024]{1,0:T(4,128)} %get-tuple-element.58) | copy-start | bytes 49156
  108.4 69.9 %copy-start.6 = (f32[1,1024]{1,0:T(1,128)S(1)}, f32[1,1024]{1,0:T(1,128)}, u32[]{:S(2)}) copy-start(f32[1,1024]{1,0:T(1,128)} %get-tuple-element.59) | copy-start | bytes 12292
  247.5 5.3 %copy-start.3 = (bf16[3,8,2,64,256]{4,3,2,1,0:T(8,128)(2,1)S(1)}, bf16[3,8,2,64,256]{4,3,2,1,0:T(8,128)(2,1)}, u32[]{:S(2)}) copy-start(bf16[3,8,2,64,256]{4,3,2,1,0:T(8,128)(2,1)} %get-tuple-element.68) | copy-start | bytes 4718596
  252.8 2.2 copy-start
  252.8 3.4 %copy-start.1 = (bf16[8,2,64,1024]{3,2,1,0:T(8,128)(2,1)S(1)}, bf16[8,2,64,1024]{3,2,1,0:T(8,128)(2,1)}, u32[]{:S(2)}) copy-start(bf16[8,2,64,1024]{3,2,1,0:T(8,128)(2,1)} %get-tuple-element.70) | copy-start | bytes 6291460
  256.1 4.7 %copy-start.4 = (bf16[512,1024]{1,0:T(8,128)(2,1)S(1)}, bf16[512,1024]{1,0:T(8,128)(2,1)}, u32[]{:S(2)}) copy-start(bf16[512,1024]{1,0:T(8,128)(2,1)} %get-tuple-element.95) | copy-start | bytes 3145732
  260.8 2.0 copy-start.2
where the time goes:
time: 265 us; the launch traced here: 264 us
  Pallas kernels  245 us (92%)
  local copies, waits for them, and re-layouts  10.1 us (4%)
  other arithmetic  8.58 us (3%)
    pallas_call x1, Pallas kernels, backward(): pl.pallas_call(functools.partial(bwd_kernel, n), in_specs=[anyspace] * 13...  69.2 us
    pallas_call x1, Pallas kernels, ring_sum(): pl.pallas_call(functools.partial(ring_kernel, n), in_specs=[vmem] * 3 + [...  67.9 us
    pallas_call x1, Pallas kernels, ff(): pl.pallas_call(functools.partial(ff_kernel, n), in_specs=[anyspace] * 5 +...  58.2 us
    pallas_call x1, Pallas kernels, forward(): pl.pallas_call(functools.partial(fwd_kernel, n), in_specs=[vmem] * 8 + [a...  49.6 us
    unnamed x18, local copies, waits for them, and re-layouts  6.07 us

commit v1 on v0

--- a/solution.py
+++ b/solution.py
@@ -15,7 +15,6 @@
 F32 = jnp.float32
 SCALE = HD ** (-0.5)
 MESH_ID = pl.DeviceIdType.MESH
-EARLY = 1
 AHEAD = 4
 NT = (((1,), (1,)), ((), ()))
 TN = (((0,), (0,)), ((), ()))
@@ -121,6 +120,13 @@
     def slab_rows(chunk):
         return pl.ds(pl.multiple_of(chunk * slab, slab), slab)
 
+    mix_slab = wm_hbm.shape[0] // n
+    around = mix_slab % 16 == 0
+    streams = 4 if around else 3
+
+    def mix_rows(chunk):
+        return pl.ds(pl.multiple_of(chunk * mix_slab, mix_slab), mix_slab)
+
     def piece():
         return remote(wq_hbm.at[:, slab_rows(mine)], wqf_ref.at[:, slab_rows(mine)], 0, far)
 
@@ -134,6 +140,8 @@
         return remote(rows1_ref.at[own_half(c)], rows1_ref.at[own_half(c)], 2 + c, sib)
 
     def mix_across():
+        if around:
+            return remote(wm_hbm.at[mix_rows(mine)], wmf_ref.at[mix_rows(mine)], 4, far)
         return remote(wm_hbm, wmf_ref, 4, far)
 
     def og_across(c):
@@ -158,9 +166,13 @@
     def og_own():
         return pltpu.make_async_copy(og_ref, oga_ref.at[pl.ds(0, rows)], local.at[0])
 
-    def hop(k, d, s):
+    reach = n // 2
+
+    def hop(k, d, s, part=False):
         chunk = ring_index(pos - s if d == 0 else pos + s, n)
-        ref = wqf_ref.at[k, slab_rows(chunk), d * wide : (d + 1) * wide]
+        side = width // 2 if k == 3 else wide
+        lanes = slice(d * side, (d + 1) * side) if part else slice(None)
+        ref = wmf_ref.at[mix_rows(chunk), lanes] if k == 3 else wqf_ref.at[k, slab_rows(chunk), lanes]
         return pltpu.make_async_remote_copy(
             src_ref=ref,
             dst_ref=ref,
@@ -171,13 +183,22 @@
         )
 
     def tick(s):
+        for k in range(streams):
+            for d in range(2):
+                hop(k, d, s).wait()
+
+                @pl.when(s < reach - 2)
+                def _():
+                    hop(k, d, s + 1).start()
+
+                @pl.when(s == reach - 2)
+                def _():
+                    hop(k, d, s + 1, True).start()
+
+    def last_tick():
         for k in range(3):
             for d in range(2):
-                hop(k, d, s).wait()
-
-                @pl.when(s < n - 2)
-                def _():
-                    hop(k, d, s + 1).start()
+                hop(k, d, reach - 1, True).wait()
 
     def put(k):
         near = pl.ds(0, cols3)
@@ -198,6 +219,8 @@
         return pltpu.make_async_copy(src, dst, out.at[k])
 
     piece().start()
+    if around:
+        mix_across().start()
     bias_across().start()
     loads = (
         pltpu.make_async_copy(wq_hbm, w_all.at[0], local.at[1]),
@@ -219,7 +242,12 @@
     for k in range(3):
         for d in range(2):
             hop(k, d, 0).start()
-    mix_across().start()
+    if around:
+        mix_across().wait()
+        for d in range(2):
+            hop(3, d, 0).start()
+    else:
+        mix_across().start()
     for c in range(2):
         og_across(c).start()
     og_beside().start()
@@ -239,7 +267,7 @@
     put(0).start()
     masks = half_masks()
     pairs = cols // PAIR
-    ticks = 1 + 2 * pairs
+    ticks = 1 + pairs
 
     @pl.loop(0, 2 * pairs)
     def _(p):
@@ -247,10 +275,11 @@
 
         @pl.when(p == pairs)
         def _():
-            @pl.loop(ticks, n - 1)
+            @pl.loop(ticks, reach - 1)
             def _(s):
                 tick(s)
 
+            last_tick()
             bias_across().wait()
             fill_shift(1, bqf)
             put(3).start()
@@ -294,13 +323,17 @@
                 outs.append(dot(vt[h * HD : (h + 1) * HD, :keys], e[:, side]) * inverse[:, side])
             att_ref[at, pl.ds(pl.multiple_of(p * PAIR, PAIR), PAIR)] = jnp.concatenate(outs, axis=0).T.astype(BF)
             off += keys
-            if i % 2 == 1:
+            if i == blocks - 1:
 
                 @pl.when(p < pairs)
                 def _():
-                    tick(1 + 2 * p + i // 2)
-
-    mix_across().wait()
+                    tick(1 + p)
+
+    if around:
+        for d in range(2):
+            hop(3, d, reach - 1, True).wait()
+    else:
+        mix_across().wait()
     put(4).start()
     put(5).start()
     nb = 256
@@ -383,8 +416,8 @@
             pltpu.VMEM((rows, width), BF),
             pltpu.SemaphoreType.DMA((11,)),
             pltpu.SemaphoreType.DMA((11,)),
-            pltpu.SemaphoreType.DMA((3, 2)),
-            pltpu.SemaphoreType.DMA((3, 2, n - 1)),
+            pltpu.SemaphoreType.DMA((4, 2)),
+            pltpu.SemaphoreType.DMA((4, 2, n // 2)),
             pltpu.SemaphoreType.DMA((3,)),
             pltpu.SemaphoreType.DMA((10,)),
         ],
@@ -513,9 +546,10 @@
             for d in range(2):
                 gather(kind, d, 0).start()
 
-    for kind in range(2):
-        for d in range(2):
-            ring_copy(carry_hbm.at[kind, d], kind, d, EARLY).start()
+    for d in range(2):
+        ring_copy(eg_hbm.at[part(d, 0), d], 1, d, 0).start()
+    for d in range(2):
+        ring_copy(carry_hbm.at[d], 0, d, 1).start()
 
     fill_bias(seg_ref, me // 2, bias_ref, blocks)
     masks = half_masks()
@@ -526,7 +560,7 @@
     ag[...] = dot(mg[...], wmf[...], NT).astype(BF)
 
     turns = 2 * pairs * blocks
-    reduce_turns = 2 * (n - 1 - EARLY)
+    reduce_turns = 2 * (n - 1) - 1
     inside = reduce_turns < turns
     hops = [(h % 2, h // 2) for h in range(max(turns - reduce_turns - 1, 0), 2 * AHEAD)]
     if not inside:
@@ -583,7 +617,7 @@
 
             @pl.when(turn < reduce_turns)
             def _():
-                tick(i % 2, EARLY + turn // 2)
+                tick((i + 1) % 2, (turn + 1) // 2)
 
             if inside and i == reduce_turns % blocks:
 
@@ -596,7 +630,7 @@
 
                 @pl.when(jnp.logical_and(hop >= 0, hop < 2 * AHEAD))
                 def _():
-                    gather_tick((i + 1) % 2, hop // 2)
+                    gather_tick(i % 2, hop // 2)
         dv = dv_ref[...].astype(BF)
         dqkv[:, lanes(1)] = dk_ref[...].astype(BF)
         dqkv[:, lanes(2)] = dv
@@ -620,12 +654,13 @@
                 q_send[k] = dot(rows1[...], dqkv[:, to], TN).astype(BF)
                 q_across(k).start()
 
-    @pl.loop(EARLY + blocks * pairs, n - 1)
-    def _(s):
-        for kind in range(2):
-            tick(kind, s)
-
     if not inside:
+        tick(1, turns // 2)
+
+        @pl.loop(turns // 2 + 1, n - 1)
+        def _(s):
+            for kind in range(2):
+                tick(kind, s)
         gather_begin()
     for k in (8, 9):
         load(k).wait()
@@ -925,29 +960,15 @@
     def part_of(d, s):
         return ring_index(pos - 1 - s if d == 0 else pos + 1 + s, n)
 
-    def ring_copy(src, kind, d, s):
+    def ring_copy(src, d):
         return pltpu.make_async_remote_copy(
             src_ref=src,
-            dst_ref=rbuf.at[s, kind, d],
-            send_sem=ring_send.at[kind, d],
-            recv_sem=ring_recv.at[kind, d, s],
+            dst_ref=rbuf.at[d],
+            send_sem=ring_send.at[d],
+            recv_sem=ring_recv.at[d],
             device_id={"dp": sides[d]},
             device_id_type=MESH_ID,
         )
-
-    ffg = (rg_ref, eg_ref)
-
-    def ring_start(kind):
-        for d in range(2):
-            ring_copy(ffg[kind].at[part_of(d, 0), d], kind, d, 0).start()
-
-    def tick(kind, s):
-        for d in range(2):
-            ring_copy(rbuf.at[s, kind, d], kind, d, s).wait()
-            total = rbuf[s, kind, d].astype(F32) + ffg[kind][part_of(d, s + 1), d].astype(F32)
-            rbuf[s, kind, d] = total.astype(BF)
-            if s + 1 < EARLY:
-                ring_copy(rbuf.at[s, kind, d], kind, d, s + 1).start()
 
     @pl.loop(0, width // nb)
     def _(k):
@@ -955,7 +976,8 @@
         grad = dot(act[...], og_ref[:, cols], TN).astype(BF)
         rg_ref[:, :, :, cols] = grad.reshape(n, 2, h, nb)
 
-    ring_start(0)
+    for d in range(2):
+        ring_copy(rg_ref.at[part_of(d, 0), d], d).start()
     put(0).start()
 
     @pl.loop(0, width // nb)
@@ -964,7 +986,6 @@
         grad = dot(n2b[...], pg[:, cols], TN).astype(BF)
         eg_ref[:, :, :, cols] = grad.reshape(n, 2, h, nb)
 
-    ring_start(1)
     put(1).start()
     br_beside().wait()
     brn_ref[...] = (br[0:rows, :].astype(F32) + br_s[...].astype(F32)).astype(BF)
@@ -1005,12 +1026,10 @@
         mg_beside(c).start()
         put(4 + c).start()
         put(6 + c).start()
-        if c == 0:
-            for s in range(EARLY):
-                tick(0, s)
-    for s in range(EARLY):
-        tick(1, s)
-    carry_ref[...] = rbuf[EARLY - 1]
+
+    for d in range(2):
+        ring_copy(rg_ref.at[part_of(d, 0), d], d).wait()
+        carry_ref[d] = (rbuf[d].astype(F32) + rg_ref[part_of(d, 1), d].astype(F32)).astype(BF)
     for c in range(2):
         mg_beside(c).wait()
     for k in range(8):
@@ -1036,7 +1055,7 @@
             jax.ShapeDtypeStruct((rows, width), BF),
             jax.ShapeDtypeStruct((1, units), F32),
             jax.ShapeDtypeStruct((4, width), F32),
-            jax.ShapeDtypeStruct((2, 2, units // (2 * n), width), BF),
+            jax.ShapeDtypeStruct((2, units // (2 * n), width), BF),
         ],
         scratch_shapes=[
             pltpu.VMEM((rows, width), F32),
@@ -1060,11 +1079,11 @@
             pltpu.VMEM((rows, width), BF),
             pltpu.VMEM((2, part, width), BF),
             pltpu.VMEM((2, part, width), BF),
-            pltpu.VMEM((EARLY, 2, 2, units // (2 * n), width), BF),
+            pltpu.VMEM((2, units // (2 * n), width), BF),
             pltpu.SemaphoreType.DMA((15,)),
             pltpu.SemaphoreType.DMA((15,)),
-            pltpu.SemaphoreType.DMA((2, 2)),
-            pltpu.SemaphoreType.DMA((2, 2, EARLY)),
+            pltpu.SemaphoreType.DMA((2,)),
+            pltpu.SemaphoreType.DMA((2,)),
             pltpu.SemaphoreType.DMA((6,)),
             pltpu.SemaphoreType.DMA((8,)),
         ],
@@ -1076,9 +1095,9 @@
 
 
 def ring_kernel(
-    n, g_ref, small_ref, rbias_ref, resid_hbm, brn_hbm, brf_hbm, _r, _e,
+    n, g_ref, norm_ref, dsum_ref, usum_ref, qsum_ref, rbias_ref, resid_hbm, brn_hbm, brf_hbm, _r, _e,
     qo_ref, mo_ref, ro_ref, eo_ref, so_ref, bo_ref,
-    buf, sbuf, sall, speer, ssum, resid, brn, bro,
+    buf, rows8, small_ref, sbuf, sall, speer, ssum, resid, brn, bro,
     send, recv, fsend, frecv, ssend, srecv, tsend, trecv, local,
 ):
     mine, pos, sides = ring_place(n)
@@ -1092,6 +1111,22 @@
     for load in loads:
         load.start()
     meet(peers, sides)
+
+    cols = qsum_ref.shape[1]
+    piece = small_ref.shape[2]
+    per = rows8.shape[1] // piece
+    rows8[0:2] = norm_ref[...]
+    rows8[2:6] = dsum_ref[...]
+    rows8[6:7] = usum_ref[...]
+    rows8[7:8] = jnp.zeros_like(rows8[7:8])
+    for k in range(2):
+        rows8[7:8, k * cols : (k + 1) * cols] = qsum_ref[k : k + 1, :]
+
+    def in_row(c):
+        return slice(c // per, c // per + 1), slice(c % per * piece, (c % per + 1) * piece)
+
+    for c in range(n):
+        small_ref[c] = rows8[in_row(c)]
 
     def remote(src, dst, kind, d, s):
         return pltpu.make_async_remote_copy(
@@ -1258,30 +1293,34 @@
     for k, d in streams:
         gather(k, d, last).wait()
     gather_small(last).wait()
-    so_ref[...] = sall[...]
+    for c in range(n):
+        so_ref[in_row(c)] = sall[c]
     beside_step(1, last, finish)
 
 
-def ring_sum(g, small, resid, brn, brf, r, e, rbias, n):
+def ring_sum(g, norm, dsum, usum, qsum, resid, brn, brf, r, e, rbias, n):
     split = (4, n, 2, g.shape[1] // (2 * n), g.shape[2])
-    s3 = small.reshape(n, 1, small.size // n)
+    s3 = jax.ShapeDtypeStruct((n, 1, 8 * norm.shape[1] // n), F32)
+    small = jax.ShapeDtypeStruct((8, norm.shape[1]), F32)
     vmem = pl.BlockSpec(memory_space=pltpu.VMEM)
     anyspace = pl.BlockSpec(memory_space=pl.ANY)
     qo, mo, ro, eo, so, bo = pl.pallas_call(
         functools.partial(ring_kernel, n),
-        in_specs=[vmem] * 3 + [anyspace] * 5,
+        in_specs=[vmem] * 6 + [anyspace] * 5,
         out_specs=[anyspace] * 4 + [vmem] * 2,
-        input_output_aliases={6: 2, 7: 3},
+        input_output_aliases={9: 2, 10: 3},
         out_shape=[
             jax.ShapeDtypeStruct((3,) + split[1:], BF),
             jax.ShapeDtypeStruct(split[1:], BF),
             jax.ShapeDtypeStruct(r.shape, BF),
             jax.ShapeDtypeStruct(e.shape, BF),
-            jax.ShapeDtypeStruct(s3.shape, F32),
+            small,
             jax.ShapeDtypeStruct(brf.shape, BF),
         ],
         scratch_shapes=[
             pltpu.VMEM((n - 1, 2, 4) + split[3:], BF),
+            pltpu.VMEM(small.shape, F32),
+            pltpu.VMEM(s3.shape, F32),
             pltpu.VMEM((n - 1,) + s3.shape[1:], F32),
             pltpu.VMEM(s3.shape, F32),
             pltpu.VMEM((3,) + s3.shape, F32),
@@ -1303,16 +1342,112 @@
             collective_id=1, has_side_effects=True, vmem_limit_bytes=60 << 20
         ),
         name="ring_sum",
-    )(g.reshape(split), s3, rbias, resid, brn, brf, r, e)
+    )(g.reshape(split), norm, dsum, usum, qsum, rbias, resid, brn, brf, r, e)
     wide = (-1, r.shape[-1])
     return (
         qo.reshape((3,) + g.shape[1:]),
         mo.reshape(g.shape[1:]),
         ro.reshape(wide),
         eo.reshape(wide),
-        so.reshape(small.shape),
+        so,
         bo,
     )
+
+
+def finish_kernel(
+    q_hbm, m_hbm, r_hbm, e_hbm, in_hbm, bo_hbm, small_ref,
+    bo_out, in_out, q_out, m_out, r_out, e_out, g1_ref, s1_ref, mb_ref, g2_ref, s2_ref, rb_ref, eb_ref, qb_ref,
+    q_in, m_in, r_in, e_in, q_wide, m_wide, r_wide, e_wide, in_mid, bo_mid, read, write,
+):
+    enter = (
+        pltpu.make_async_copy(in_hbm, in_mid, read.at[12]),
+        pltpu.make_async_copy(bo_hbm, bo_mid, read.at[13]),
+    )
+    leave = (
+        pltpu.make_async_copy(in_mid, in_out, write.at[0]),
+        pltpu.make_async_copy(bo_mid, bo_out, write.at[1]),
+    )
+    quarter = r_in.shape[0] // 4
+    jobs = []
+    for c in range(4):
+        at = pl.ds(c * quarter, quarter)
+        for src, mid, wide, dst in ((r_hbm, r_in, r_wide, r_out), (e_hbm, e_in, e_wide, e_out)):
+            jobs.append((src.at[at], mid.at[at], wide.at[at], dst.at[at]))
+    for k in range(3):
+        jobs.append((q_hbm.at[k], q_in.at[k], q_wide.at[k], q_out.at[k]))
+    gets = [pltpu.make_async_copy(job[0], job[1], read.at[k]) for k, job in enumerate(jobs)]
+    get_m = pltpu.make_async_copy(m_hbm, m_in, read.at[len(jobs)])
+    get_m.start()
+    for copy in enter:
+        copy.start()
+    for get in gets:
+        get.start()
+    for k, ref in enumerate((g1_ref, s1_ref, mb_ref, g2_ref, s2_ref, rb_ref, eb_ref)):
+        ref[...] = small_ref[k : k + 1, :]
+    cols = qb_ref.shape[1]
+    for k in range(2):
+        qb_ref[k : k + 1, :] = small_ref[7:8, k * cols : (k + 1) * cols]
+    for k in range(2):
+        enter[k].wait()
+        leave[k].start()
+    get_m.wait()
+    m_wide[...] = m_in[...].astype(F32).T
+    puts = [pltpu.make_async_copy(m_wide, m_out, write.at[2])]
+    puts[0].start()
+    for k, (_src, mid, wide, dst) in enumerate(jobs):
+        gets[k].wait()
+        step = 64
+
+        @pl.loop(0, mid.shape[0] // step)
+        def _(r):
+            at = pl.ds(pl.multiple_of(r * step, step), step)
+            wide[at] = mid[at].astype(F32)
+
+        put = pltpu.make_async_copy(wide, dst, write.at[3 + k])
+        put.start()
+        puts.append(put)
+    for copy in leave:
+        copy.wait()
+    for put in puts:
+        put.wait()
+
+
+def finish(q, m, r, e, in_grad, block_out, small):
+    vmem = pl.BlockSpec(memory_space=pltpu.VMEM)
+    anyspace = pl.BlockSpec(memory_space=pl.ANY)
+    width = small.shape[1]
+    row = jax.ShapeDtypeStruct((1, width), F32)
+    return pl.pallas_call(
+        finish_kernel,
+        in_specs=[anyspace] * 6 + [vmem],
+        out_specs=[anyspace] * 6 + [vmem] * 8,
+        out_shape=[
+            jax.ShapeDtypeStruct(block_out.shape, BF),
+            jax.ShapeDtypeStruct(in_grad.shape, F32),
+            jax.ShapeDtypeStruct(q.shape, F32),
+            jax.ShapeDtypeStruct(m.shape[::-1], F32),
+            jax.ShapeDtypeStruct(r.shape, F32),
+            jax.ShapeDtypeStruct(e.shape, F32),
+        ]
+        + [row] * 7
+        + [jax.ShapeDtypeStruct((2, q.shape[2]), F32)],
+        scratch_shapes=[
+            pltpu.VMEM(q.shape, BF),
+            pltpu.VMEM(m.shape, BF),
+            pltpu.VMEM(r.shape, BF),
+            pltpu.VMEM(e.shape, BF),
+            pltpu.VMEM(q.shape, F32),
+            pltpu.VMEM(m.shape[::-1], F32),
+            pltpu.VMEM(r.shape, F32),
+            pltpu.VMEM(e.shape, F32),
+            pltpu.VMEM(in_grad.shape, F32),
+            pltpu.VMEM(block_out.shape, BF),
+            pltpu.SemaphoreType.DMA((14,)),
+            pltpu.SemaphoreType.DMA((14,)),
+        ],
+        compiler_params=pltpu.CompilerParams(vmem_limit_bytes=60 << 20),
+        name="finish",
+    )(q, m, r, e, in_grad, block_out, small)
 
 
 def body(
@@ -1373,18 +1508,12 @@
         first_gain.reshape(flat),
         dp_size,
     )
-    small = jnp.concatenate(
-        [
-            norm_sums,
-            sums2,
-            unit_sums,
-            jnp.pad(qv_sums.reshape(1, 2 * cols), ((0, 0), (0, width - 2 * cols))),
-        ],
-        axis=0,
-    )
     qkv_grad, mix_grad, reduce_all, expand_all, small, block_out = ring_sum(
         grads,
-        small,
+        norm_sums,
+        sums2,
+        unit_sums,
+        qv_sums,
         resid,
         br_near,
         br_far,
@@ -1393,21 +1522,25 @@
         reduce_bias.reshape(flat),
         dp_size,
     )
+    block_out, in_grad, qkv_grad, mix_grad, reduce_all, expand_all, *rest, qv_bias_grad = finish(
+        qkv_grad, mix_grad, reduce_all, expand_all, in_grad, block_out, small
+    )
+    g1, s1, mb, g2, s2, rb, eb = (item.reshape(-1) for item in rest)
     return (
         block_out,
         in_grad,
-        small[0],
-        small[1],
-        qkv_grad.astype(F32).transpose(1, 0, 2),
-        small[7, : 2 * cols].reshape(2, cols),
-        mix_grad.astype(F32).T,
-        small[2],
-        small[3],
-        small[4],
-        expand_all.astype(F32),
-        small[6],
-        reduce_all.astype(F32),
-        small[5],
+        g1,
+        s1,
+        qkv_grad.transpose(1, 0, 2),
+        qv_bias_grad,
+        mix_grad,
+        mb,
+        g2,
+        s2,
+        expand_all,
+        eb,
+        reduce_all,
+        rb,
     )
 
 

time: 265 us -> 254 us (0.958)
  local copies, waits for them, and re-layouts: 10.1 us -> 0 us
  other arithmetic: 8.58 us -> 0 us
  Pallas kernels: 245 us -> 252 us
    pallas_call x1 -> x2, Pallas kernels: 67.9 us -> 77.3 us  [the longest x1 67.8 us: ring_sum(): pl.pallas_call(functools.partial(ring_kernel, n), in_specs=[vmem] * 6 + [...]
    unnamed x18 -> x0, local copies, waits for them, and re-layouts: 6.07 us -> none
    convert_element_type x1 -> x0, other arithmetic: 4.72 us -> none  [body(): reduce_all.astype(F32)]
    transpose x2 -> x0, other arithmetic: 3.14 us -> none  [the longest x1 2.03 us: body(): qkv_grad.astype(F32).transpose(1, 0, 2)]
where the time goes in v1:
time: 254 us; the launch traced here: 253 us
  Pallas kernels  252 us (99%)
    pallas_call x1, Pallas kernels, backward(): pl.pallas_call(functools.partial(bwd_kernel, n), in_specs=[anyspace] * 13...  70.2 us
    pallas_call x1, Pallas kernels, ring_sum(): pl.pallas_call(functools.partial(ring_kernel, n), in_specs=[vmem] * 6 + [...  67.8 us
    pallas_call x1, Pallas kernels, ff(): pl.pallas_call(functools.partial(ff_kernel, n), in_specs=[anyspace] * 5 +...  58 us
    pallas_call x1, Pallas kernels, forward(): pl.pallas_call(functools.partial(fwd_kernel, n), in_specs=[vmem] * 8 + [a...  47 us
    pallas_call x1, Pallas kernels, finish(): pl.pallas_call(finish_kernel, in_specs=[anyspace] * 6 + [vmem], out_specs...  9.48 us

profile of v1, /device:TPU:0, one launch (start us, length us, event | category | flops | bytes accessed | tf_op | source)
XLA Modules:
  0.0 253.4 jit_solution(2832008837401998502)
XLA Ops:
  0.6 47.0 %forward.1 = (bf16[1024,1024]{1,0:T(8,128)(2,1)}, bf16[1024,1536]{1,0:T(8,128)(2,1)}, bf16[1024,512]{1,0:T(8,128)(2,1)}, f32[512,1024]{1,0:T(8,128)}, bf16[512,1...) custom-call(bf16[512,1024]{1,0:T(8,128)(2,1)} %x_hbm.1, ...), custom_call_target="tpu_custom_call" | custom-call | tf_op jit(solution)/shard_map/forward/pallas_call | solution.py:390
  47.7 58.0 %ff.1 = (f32[512,1024]{1,0:T(8,128)}, bf16[1024,1024]{1,0:T(8,128)(2,1)}, bf16[8,2,64,1024]{3,2,1,0:T(8,128)(2,1)}, bf16[8,2,64,1024]{3,2,1,0:T(8,128)(2,1)}, bf...) custom-call(bf16[512,1024]{1,0:T(8,128)(2,1)} %get-tuple-element.57., ...), custom_call_target="tpu_custom_call" | custom-call | tf_op jit(solution)/shard_map/ff/pallas_call | solution.py:1045
  105.6 70.2 %backward.1 = (f32[512,1024]{1,0:T(8,128)}, bf16[4,1024,256]{2,1,0:T(8,128)(2,1)}, f32[2,256]{1,0:T(2,128)}, f32[2,1024]{1,0:T(2,128)}, bf16[8,2,64,1024]{3,2,1,...) custom-call(bf16[1024,1024]{1,0:T(8,128)(2,1)} %get-tuple-element.60.mg_hbm, bf16[1024,1536]{1,0:T(8,128)(2,1)} %get-tuple-element.61.qkv_hbm, ...), custom_call_target="tpu_custom_call" | custom-call | tf_op jit(solution)/shard_map/backward/pallas_call | solution.py:742
  175.9 67.8 %ring_sum.1 = (bf16[3,8,2,64,256]{4,3,2,1,0:T(8,128)(2,1)}, bf16[8,2,64,256]{3,2,1,0:T(8,128)(2,1)}, bf16[8,2,64,1024]{3,2,1,0:T(8,128)(2,1)}, bf16[8,2,64,1024]...) custom-call(bf16[4,8,2,64,256]{4,3,2,1,0:T(8,128)(2,1)} %bitcast.25,, ...), custom_call_target="tpu_custom_call", output_to_operand_aliasing={{2}: (9, {}), {3}: (10, {})} | custom-call | tf_op jit(solution)/shard_map/ring_sum/pallas_call | solution.py:1307
  243.7 9.5 %finish.1 = (bf16[512,1024]{1,0:T(8,128)(2,1)}, f32[512,1024]{1,0:T(8,128)}, f32[3,1024,256]{2,1,0:T(8,128)}, f32[256,1024]{1,0:T(8,128)}, f32[1024,1024]{1,0:T(...) custom-call(bf16[3,1024,256]{2,1,0:T(8,128)(2,1)} %bitcast.26, ...), custom_call_target="tpu_custom_call" | custom-call | tf_op jit(solution)/shard_map/finish/pallas_call | solution.py:1420

commit v2 on v1

--- a/solution.py
+++ b/solution.py
@@ -15,7 +15,7 @@
 F32 = jnp.float32
 SCALE = HD ** (-0.5)
 MESH_ID = pl.DeviceIdType.MESH
-AHEAD = 4
+AHEAD = 3
 NT = (((1,), (1,)), ((), ()))
 TN = (((0,), (0,)), ((), ()))
 
@@ -428,15 +428,220 @@
     )(x, segments, g1, s1, bq, mixb, g2, s2, wq, wm, og)
 
 
+def ring_part(
+    n, between, g_ref, norm_ref, qsum_ref, dsum_ref, usum_ref, rbias_ref, resid_hbm, brn_hbm, brf_hbm,
+    qo_ref, mo_ref, ro_ref, eo_ref, so_ref, bo_ref,
+    buf, rows8, small_ref, sbuf, sall, speer, ssum, resid, brn, bro,
+    send, recv, fsend, frecv, ssend, srecv, tsend, trecv, local,
+):
+    mine, pos, sides = ring_place(n)
+    me = lax.axis_index("tensor")
+    far = (me + 2) % 4
+    peers = [(me + k) % 4 for k in range(1, 4)]
+    loads = (
+        pltpu.make_async_copy(resid_hbm, resid, local.at[0]),
+        pltpu.make_async_copy(brn_hbm, brn, local.at[1]),
+    )
+    for load in loads:
+        load.start()
+
+    cols = qsum_ref.shape[1]
+    piece = small_ref.shape[2]
+    per = rows8.shape[1] // piece
+    rows8[0:2] = norm_ref[...]
+    rows8[2:6] = dsum_ref[...]
+    rows8[6:7] = usum_ref[...]
+    rows8[7:8] = jnp.zeros_like(rows8[7:8])
+    for k in range(2):
+        rows8[7:8, k * cols : (k + 1) * cols] = qsum_ref[k : k + 1, :]
+
+    def in_row(c):
+        return slice(c // per, c // per + 1), slice(c % per * piece, (c % per + 1) * piece)
+
+    for c in range(n):
+        small_ref[c] = rows8[in_row(c)]
+
+    def remote(src, dst, kind, d, s):
+        return pltpu.make_async_remote_copy(
+            src_ref=src,
+            dst_ref=dst,
+            send_sem=send.at[kind, d],
+            recv_sem=recv.at[kind, d, s],
+            device_id={"dp": sides[d]},
+            device_id_type=MESH_ID,
+        )
+
+    def little(src, dst, kind, s):
+        return pltpu.make_async_remote_copy(
+            src_ref=src,
+            dst_ref=dst,
+            send_sem=ssend.at[kind],
+            recv_sem=srecv.at[kind, s],
+            device_id={"dp": sides[0]},
+            device_id_type=MESH_ID,
+        )
+
+    def beside(src, dst, k, other):
+        return pltpu.make_async_remote_copy(
+            src_ref=src,
+            dst_ref=dst,
+            send_sem=tsend.at[k],
+            recv_sem=trecv.at[k],
+            device_id={"tensor": other},
+            device_id_type=MESH_ID,
+        )
+
+    def share(k):
+        return beside(small_ref, speer.at[k], k, peers[k])
+
+    def branch():
+        return beside(brf_hbm, bro, 3, far)
+
+    def part(d, s):
+        return ring_index(pos - 1 - s if d == 0 else pos + 1 + s, n)
+
+    def held(d, s):
+        return ring_index(pos - s if d == 0 else pos + s, n)
+
+    streams = [(k, d) for k in range(4) for d in range(2)]
+
+    def source(k, chunk, d):
+        return g_ref.at[k, chunk, d]
+
+    def slot(k, s, d):
+        return buf.at[s, d, k]
+
+    def put_at(k, chunk, d):
+        return qo_ref.at[k, chunk, d] if k < 3 else mo_ref.at[chunk, d]
+
+    def add(k, d, s):
+        ref = slot(k, s, d)
+        total = ref[...].astype(F32) + source(k, part(d, s + 1), d)[...].astype(F32)
+        ref[...] = total.astype(BF)
+
+    def gather(k, d, s):
+        ref = put_at(k, held(d, s), d)
+        return remote(ref, ref, 4 + k, d, s)
+
+    left = n - 1 - AHEAD
+    half = ro_ref.shape[3] // 2
+
+    def ff_hop(kind, c, d, s):
+        ref = (ro_ref, eo_ref)[kind].at[held(d, s), d, :, pl.ds(c * half, half)]
+        k = 2 * kind + c
+        return pltpu.make_async_remote_copy(
+            src_ref=ref,
+            dst_ref=ref,
+            send_sem=fsend.at[k, d],
+            recv_sem=frecv.at[k, d, s - AHEAD],
+            device_id={"dp": sides[d]},
+            device_id_type=MESH_ID,
+        )
+
+    def beside_step(kind, s, act):
+        @pl.when(s < left)
+        def _():
+            for d in range(2):
+                act(ff_hop(kind, 0, d, AHEAD + s))
+
+        @pl.when(s >= n - 1 - left)
+        def _():
+            for d in range(2):
+                act(ff_hop(kind, 1, d, AHEAD + s - (n - 1 - left)))
+
+    def start(copy):
+        copy.start()
+
+    def finish(copy):
+        copy.wait()
+
+    def gather_small(s):
+        ref = sall.at[held(0, s)]
+        return little(ref, ref, 1, s)
+
+    for k, d in streams:
+        remote(source(k, part(d, 0), d), slot(k, 0, d), k, d, 0).start()
+    for k in range(3):
+        share(k).start()
+    branch().start()
+    between()
+    for k in range(3):
+        share(k).wait()
+    ssum[...] = small_ref[...]
+    shared = n * 6 // 8
+    ssum[0:shared] = ssum[0:shared] + speer[0, 0:shared] + speer[1, 0:shared] + speer[2, 0:shared]
+    little(ssum.at[part(0, 0)], sbuf.at[0], 0, 0).start()
+
+    @pl.loop(0, n - 2)
+    def _(s):
+        beside_step(0, s, start)
+        for k, d in streams:
+            remote(slot(k, s, d), slot(k, s, d), k, d, s).wait()
+            add(k, d, s)
+            remote(slot(k, s, d), slot(k, s + 1, d), k, d, s + 1).start()
+        little(sbuf.at[s], sbuf.at[s], 0, s).wait()
+        sbuf[s] = sbuf[s] + ssum[part(0, s + 1)]
+        little(sbuf.at[s], sbuf.at[s + 1], 0, s + 1).start()
+        beside_step(0, s, finish)
+
+    last = n - 2
+    beside_step(0, last, start)
+    puts = []
+    for k, d in streams:
+        remote(slot(k, last, d), slot(k, last, d), k, d, last).wait()
+        add(k, d, last)
+        put = pltpu.make_async_copy(slot(k, last, d), put_at(k, mine, d), local.at[2 + 2 * k + d])
+        put.start()
+        puts.append(put)
+    for (k, d), put in zip(streams, puts):
+        put.wait()
+        gather(k, d, 0).start()
+    little(sbuf.at[last], sbuf.at[last], 0, last).wait()
+    sall[mine] = sbuf[last] + ssum[mine]
+    gather_small(0).start()
+    beside_step(0, last, finish)
+
+    @pl.loop(0, n - 2)
+    def _(s):
+        beside_step(1, s, start)
+        for k, d in streams:
+            gather(k, d, s).wait()
+            gather(k, d, s + 1).start()
+        gather_small(s).wait()
+        gather_small(s + 1).start()
+        beside_step(1, s, finish)
+
+    beside_step(1, last, start)
+
+    branch().wait()
+    for load in loads:
+        load.wait()
+    step = 64
+
+    @pl.loop(0, bo_ref.shape[0] // step)
+    def _(r):
+        at = pl.ds(pl.multiple_of(r * step, step), step)
+        total = resid[at, :] + brn[at, :].astype(F32) + bro[at, :].astype(F32) + rbias_ref[...]
+        bo_ref[at, :] = total.astype(BF)
+
+    for k, d in streams:
+        gather(k, d, last).wait()
+    gather_small(last).wait()
+    for c in range(n):
+        so_ref[in_row(c)] = sall[c]
+    beside_step(1, last, finish)
+
+
 def bwd_kernel(
     n,
     mg_hbm, qkv_hbm, att_hbm, rows1_hbm, wq_hbm, wqf_hbm, wm_hbm, wmf_hbm, x_hbm, rgrad_hbm, rg_hbm, eg_hbm, carry_hbm,
-    seg_ref, g1_ref,
-    in_out, qg_out, qsum_ref, nsum_ref, ro_ref, eo_ref,
-    in_ref, qg_ref,
+    resid_hbm, brn_hbm, brf_hbm, seg_ref, g1_ref, dsum_ref, usum_ref, rbias_ref,
+    in_out, qo_ref, mo_ref, ro_ref, eo_ref, so_ref, bo_ref,
+    in_ref, qg_ref, qsum_ref, nsum_ref,
     mg, qkv, att, rows1, wq, wqf, wm, wmf, x, rgrad, ffg,
     rbuf, dqkv, ag, bias_ref, dk_ref, dv_ref, q_send, q_got, m_send, m_got, s_got, s_send, psend, pgot, n1g,
     send, recv, ring_send, ring_recv, gather_send, gather_recv, local, out,
+    *ring_scratch,
 ):
     rows, width = in_ref.shape
     seq = mg.shape[0]
@@ -460,7 +665,7 @@
 
     for k in range(len(pairs_in)):
         load(k).start()
-    meet((sib, far), sides)
+    meet([(me + k) % 4 for k in range(1, 4)], sides)
 
     def remote(src, dst, k, other):
         return pltpu.make_async_remote_copy(
@@ -509,10 +714,8 @@
 
     outs_hbm = (ro_ref, eo_ref)
 
-    def put(k):
-        if isinstance(k, int) and k == 4:
-            return pltpu.make_async_copy(in_ref, in_out, out.at[4])
-        return pltpu.make_async_copy(qg_ref.at[k], qg_out.at[k], out.at[k])
+    def put_in():
+        return pltpu.make_async_copy(in_ref, in_out, out.at[0])
 
     def gather(kind, d, s):
         chunk = ring_index(pos - s if d == 0 else pos + s, n)
@@ -546,10 +749,9 @@
             for d in range(2):
                 gather(kind, d, 0).start()
 
-    for d in range(2):
-        ring_copy(eg_hbm.at[part(d, 0), d], 1, d, 0).start()
-    for d in range(2):
-        ring_copy(carry_hbm.at[d], 0, d, 1).start()
+    for kind in range(2):
+        for d in range(2):
+            ring_copy(carry_hbm.at[kind, d], kind, d, 1).start()
 
     fill_bias(seg_ref, me // 2, bias_ref, blocks)
     masks = half_masks()
@@ -559,12 +761,8 @@
     m_across().start()
     ag[...] = dot(mg[...], wmf[...], NT).astype(BF)
 
-    turns = 2 * pairs * blocks
-    reduce_turns = 2 * (n - 1) - 1
-    inside = reduce_turns < turns
-    hops = [(h % 2, h // 2) for h in range(max(turns - reduce_turns - 1, 0), 2 * AHEAD)]
-    if not inside:
-        hops = [(h % 2, h // 2) for h in range(2 * AHEAD)]
+    turns = 2 * pairs + blocks * pairs
+    hops = [(kind, s) for s in range(AHEAD) for kind in range(2)]
 
     def next_hop():
         if hops:
@@ -613,24 +811,18 @@
             dqkv[at, lanes(0)] = dq
             qsum += jnp.sum(dq.astype(F32), axis=0, keepdims=True)
             off += keys
-            turn = blocks * q + i
-
-            @pl.when(turn < reduce_turns)
+            late = 2 * pairs + blocks * (q - pairs) + i
+
+            @pl.when(jnp.logical_and(q >= pairs, late < 2 * (n - 2)))
             def _():
-                tick((i + 1) % 2, (turn + 1) // 2)
-
-            if inside and i == reduce_turns % blocks:
-
-                @pl.when(turn == reduce_turns)
+                tick(i % 2, 1 + late // 2)
+
+            if i % 2 == 1:
+
+                @pl.when(first)
                 def _():
-                    gather_begin()
-
-            if inside:
-                hop = turn - reduce_turns - 1
-
-                @pl.when(jnp.logical_and(hop >= 0, hop < 2 * AHEAD))
-                def _():
-                    gather_tick(i % 2, hop // 2)
+                    tick(i // 2, 1 + q)
+
         dv = dv_ref[...].astype(BF)
         dqkv[:, lanes(1)] = dk_ref[...].astype(BF)
         dqkv[:, lanes(2)] = dv
@@ -654,14 +846,12 @@
                 q_send[k] = dot(rows1[...], dqkv[:, to], TN).astype(BF)
                 q_across(k).start()
 
-    if not inside:
-        tick(1, turns // 2)
-
-        @pl.loop(turns // 2 + 1, n - 1)
-        def _(s):
-            for kind in range(2):
-                tick(kind, s)
-        gather_begin()
+    @pl.loop(1 + turns // 2, n - 1)
+    def _(s):
+        for kind in range(2):
+            tick(kind, s)
+
+    gather_begin()
     for k in (8, 9):
         load(k).wait()
     nb = 256
@@ -706,12 +896,12 @@
         nsum_ref[0:1, :] += jnp.sum(grad * normed, axis=0, keepdims=True)
         nsum_ref[1:2, :] += jnp.sum(grad, axis=0, keepdims=True)
 
-    put(4).start()
+    put_in().start()
     next_hop()
     mixed = dot(mg[...], att[:, 0:cols], TN)
     m_across().wait()
-    qg_ref[3] = (mixed + m_got[...].astype(F32)).astype(BF)
-    put(3).start()
+    pieces = qg_ref.shape[1:]
+    qg_ref[3] = (mixed + m_got[...].astype(F32)).astype(BF).reshape(pieces)
     s_across().wait()
     qsum_ref[...] += s_got[...]
     next_hop()
@@ -721,16 +911,24 @@
         to = pl.ds(pl.multiple_of(k * cols, cols), cols)
         qg = dot(rows1[...], dqkv[:, to], TN)
         q_across(k).wait()
-        qg_ref[k] = (qg + q_got[k].astype(F32)).astype(BF)
-        put(k).start()
-
-    while hops:
-        next_hop()
-    for k in range(5):
-        put(k).wait()
-
-
-def backward(mg, qkv, att, rows1, wq, wqf, wm, wmf, x, rgrad, rg, eg, carry, segments, g1, n):
+        qg_ref[k] = (qg + q_got[k].astype(F32)).astype(BF).reshape(pieces)
+
+    def rest_of_hops():
+        while hops:
+            next_hop()
+
+    ring_part(
+        n, rest_of_hops, qg_ref, nsum_ref, qsum_ref, dsum_ref, usum_ref, rbias_ref, resid_hbm, brn_hbm, brf_hbm,
+        qo_ref, mo_ref, ro_ref, eo_ref, so_ref, bo_ref,
+        *ring_scratch,
+    )
+    put_in().wait()
+
+
+def backward(
+    mg, qkv, att, rows1, wq, wqf, wm, wmf, x, rgrad, rg, eg, carry, resid, brn, brf,
+    segments, g1, dsum, usum, rbias, n,
+):
     rows, width = x.shape
     seq = mg.shape[0]
     cols = wq.shape[2]
@@ -739,21 +937,26 @@
     anyspace = pl.BlockSpec(memory_space=pl.ANY)
     split = rg.shape
     chunk = split[2:]
-    return pl.pallas_call(
+    pieces = (4, n, 2, width // (2 * n), cols)
+    small = (n, 1, 8 * width // n)
+    in_grad, qo, mo, ro, eo, so, bo = pl.pallas_call(
         functools.partial(bwd_kernel, n),
-        in_specs=[anyspace] * 13 + [vmem] * 2,
-        out_specs=[anyspace] * 2 + [vmem] * 2 + [anyspace] * 2,
+        in_specs=[anyspace] * 16 + [vmem] * 5,
+        out_specs=[anyspace] * 5 + [vmem] * 2,
         out_shape=[
             jax.ShapeDtypeStruct((rows, width), F32),
-            jax.ShapeDtypeStruct((4, width, cols), BF),
-            jax.ShapeDtypeStruct((2, cols), F32),
-            jax.ShapeDtypeStruct((2, width), F32),
+            jax.ShapeDtypeStruct((3,) + pieces[1:], BF),
+            jax.ShapeDtypeStruct(pieces[1:], BF),
             jax.ShapeDtypeStruct(split, BF),
             jax.ShapeDtypeStruct(split, BF),
+            jax.ShapeDtypeStruct((8, width), F32),
+            jax.ShapeDtypeStruct((rows, width), BF),
         ],
         scratch_shapes=[
             pltpu.VMEM((rows, width), F32),
-            pltpu.VMEM((4, width, cols), BF),
+            pltpu.VMEM(pieces, BF),
+            pltpu.VMEM((2, cols), F32),
+            pltpu.VMEM((2, width), F32),
             pltpu.VMEM(mg.shape, BF),
             pltpu.VMEM(qkv.shape, BF),
             pltpu.VMEM(att.shape, BF),
@@ -787,13 +990,38 @@
             pltpu.SemaphoreType.DMA((2, 2)),
             pltpu.SemaphoreType.DMA((2, 2, n - 1)),
             pltpu.SemaphoreType.DMA((14,)),
-            pltpu.SemaphoreType.DMA((5,)),
+            pltpu.SemaphoreType.DMA((1,)),
+            pltpu.VMEM((n - 1, 2, 4) + pieces[3:], BF),
+            pltpu.VMEM((8, width), F32),
+            pltpu.VMEM(small, F32),
+            pltpu.VMEM((n - 1,) + small[1:], F32),
+            pltpu.VMEM(small, F32),
+            pltpu.VMEM((3,) + small, F32),
+            pltpu.VMEM(small, F32),
+            pltpu.VMEM((rows, width), F32),
+            pltpu.VMEM((rows, width), BF),
+            pltpu.VMEM((rows, width), BF),
+            pltpu.SemaphoreType.DMA((8, 2)),
+            pltpu.SemaphoreType.DMA((8, 2, n - 1)),
+            pltpu.SemaphoreType.DMA((4, 2)),
+            pltpu.SemaphoreType.DMA((4, 2, n - 1 - AHEAD)),
+            pltpu.SemaphoreType.DMA((2,)),
+            pltpu.SemaphoreType.DMA((2, n - 1)),
+            pltpu.SemaphoreType.DMA((4,)),
+            pltpu.SemaphoreType.DMA((4,)),
+            pltpu.SemaphoreType.DMA((10,)),
         ],
         compiler_params=pltpu.CompilerParams(
             collective_id=4, has_side_effects=True, vmem_limit_bytes=60 << 20
         ),
         name="backward",
-    )(mg, qkv, att, rows1, wq, wqf, wm, wmf, x, rgrad, rg, eg, carry, segments, g1)
+    )(
+        mg, qkv, att, rows1, wq, wqf, wm, wmf, x, rgrad, rg, eg, carry, resid, brn, brf,
+        segments, g1, dsum, usum, rbias,
+    )
+    wide = (-1, width)
+    mixed = mo.reshape(width, cols)
+    return in_grad, qo.reshape(3, width, cols), mixed, ro.reshape(wide), eo.reshape(wide), so, bo
 
 
 GA = 0.7978845608028654
@@ -960,12 +1188,14 @@
     def part_of(d, s):
         return ring_index(pos - 1 - s if d == 0 else pos + 1 + s, n)
 
-    def ring_copy(src, d):
+    ffg = (rg_ref, eg_ref)
+
+    def ring_copy(kind, d):
         return pltpu.make_async_remote_copy(
-            src_ref=src,
-            dst_ref=rbuf.at[d],
-            send_sem=ring_send.at[d],
-            recv_sem=ring_recv.at[d],
+            src_ref=ffg[kind].at[part_of(d, 0), d],
+            dst_ref=rbuf.at[kind, d],
+            send_sem=ring_send.at[kind, d],
+            recv_sem=ring_recv.at[kind, d],
             device_id={"dp": sides[d]},
             device_id_type=MESH_ID,
         )
@@ -977,7 +1207,7 @@
         rg_ref[:, :, :, cols] = grad.reshape(n, 2, h, nb)
 
     for d in range(2):
-        ring_copy(rg_ref.at[part_of(d, 0), d], d).start()
+        ring_copy(0, d).start()
     put(0).start()
 
     @pl.loop(0, width // nb)
@@ -986,6 +1216,8 @@
         grad = dot(n2b[...], pg[:, cols], TN).astype(BF)
         eg_ref[:, :, :, cols] = grad.reshape(n, 2, h, nb)
 
+    for d in range(2):
+        ring_copy(1, d).start()
     put(1).start()
     br_beside().wait()
     brn_ref[...] = (br[0:rows, :].astype(F32) + br_s[...].astype(F32)).astype(BF)
@@ -1027,9 +1259,11 @@
         put(4 + c).start()
         put(6 + c).start()
 
-    for d in range(2):
-        ring_copy(rg_ref.at[part_of(d, 0), d], d).wait()
-        carry_ref[d] = (rbuf[d].astype(F32) + rg_ref[part_of(d, 1), d].astype(F32)).astype(BF)
+    for kind in range(2):
+        for d in range(2):
+            ring_copy(kind, d).wait()
+            total = rbuf[kind, d].astype(F32) + ffg[kind][part_of(d, 1), d].astype(F32)
+            carry_ref[kind, d] = total.astype(BF)
     for c in range(2):
         mg_beside(c).wait()
     for k in range(8):
@@ -1055,7 +1289,7 @@
             jax.ShapeDtypeStruct((rows, width), BF),
             jax.ShapeDtypeStruct((1, units), F32),
             jax.ShapeDtypeStruct((4, width), F32),
-            jax.ShapeDtypeStruct((2, units // (2 * n), width), BF),
+            jax.ShapeDtypeStruct((2, 2, units // (2 * n), width), BF),
         ],
         scratch_shapes=[
             pltpu.VMEM((rows, width), F32),
@@ -1079,11 +1313,11 @@
             pltpu.VMEM((rows, width), BF),
             pltpu.VMEM((2, part, width), BF),
             pltpu.VMEM((2, part, width), BF),
-            pltpu.VMEM((2, units // (2 * n), width), BF),
+            pltpu.VMEM((2, 2, units // (2 * n), width), BF),
             pltpu.SemaphoreType.DMA((15,)),
             pltpu.SemaphoreType.DMA((15,)),
-            pltpu.SemaphoreType.DMA((2,)),
-            pltpu.SemaphoreType.DMA((2,)),
+            pltpu.SemaphoreType.DMA((2, 2)),
+            pltpu.SemaphoreType.DMA((2, 2)),
             pltpu.SemaphoreType.DMA((6,)),
             pltpu.SemaphoreType.DMA((8,)),
         ],
@@ -1092,266 +1326,6 @@
         ),
         name="ff",
     )(n2, og_all, we, wr, resid, be, gain)
-
-
-def ring_kernel(
-    n, g_ref, norm_ref, dsum_ref, usum_ref, qsum_ref, rbias_ref, resid_hbm, brn_hbm, brf_hbm, _r, _e,
-    qo_ref, mo_ref, ro_ref, eo_ref, so_ref, bo_ref,
-    buf, rows8, small_ref, sbuf, sall, speer, ssum, resid, brn, bro,
-    send, recv, fsend, frecv, ssend, srecv, tsend, trecv, local,
-):
-    mine, pos, sides = ring_place(n)
-    me = lax.axis_index("tensor")
-    far = (me + 2) % 4
-    peers = [(me + k) % 4 for k in range(1, 4)]
-    loads = (
-        pltpu.make_async_copy(resid_hbm, resid, local.at[0]),
-        pltpu.make_async_copy(brn_hbm, brn, local.at[1]),
-    )
-    for load in loads:
-        load.start()
-    meet(peers, sides)
-
-    cols = qsum_ref.shape[1]
-    piece = small_ref.shape[2]
-    per = rows8.shape[1] // piece
-    rows8[0:2] = norm_ref[...]
-    rows8[2:6] = dsum_ref[...]
-    rows8[6:7] = usum_ref[...]
-    rows8[7:8] = jnp.zeros_like(rows8[7:8])
-    for k in range(2):
-        rows8[7:8, k * cols : (k + 1) * cols] = qsum_ref[k : k + 1, :]
-
-    def in_row(c):
-        return slice(c // per, c // per + 1), slice(c % per * piece, (c % per + 1) * piece)
-
-    for c in range(n):
-        small_ref[c] = rows8[in_row(c)]
-
-    def remote(src, dst, kind, d, s):
-        return pltpu.make_async_remote_copy(
-            src_ref=src,
-            dst_ref=dst,
-            send_sem=send.at[kind, d],
-            recv_sem=recv.at[kind, d, s],
-            device_id={"dp": sides[d]},
-            device_id_type=MESH_ID,
-        )
-
-    def little(src, dst, kind, s):
-        return pltpu.make_async_remote_copy(
-            src_ref=src,
-            dst_ref=dst,
-            send_sem=ssend.at[kind],
-            recv_sem=srecv.at[kind, s],
-            device_id={"dp": sides[0]},
-            device_id_type=MESH_ID,
-        )
-
-    def beside(src, dst, k, other):
-        return pltpu.make_async_remote_copy(
-            src_ref=src,
-            dst_ref=dst,
-            send_sem=tsend.at[k],
-            recv_sem=trecv.at[k],
-            device_id={"tensor": other},
-            device_id_type=MESH_ID,
-        )
-
-    def share(k):
-        return beside(small_ref, speer.at[k], k, peers[k])
-
-    def branch():
-        return beside(brf_hbm, bro, 3, far)
-
-    def part(d, s):
-        return ring_index(pos - 1 - s if d == 0 else pos + 1 + s, n)
-
-    def held(d, s):
-        return ring_index(pos - s if d == 0 else pos + s, n)
-
-    streams = [(k, d) for k in range(4) for d in range(2)]
-
-    def source(k, chunk, d):
-        return g_ref.at[k, chunk, d]
-
-    def slot(k, s, d):
-        return buf.at[s, d, k]
-
-    def put_at(k, chunk, d):
-        return qo_ref.at[k, chunk, d] if k < 3 else mo_ref.at[chunk, d]
-
-    def add(k, d, s):
-        ref = slot(k, s, d)
-        total = ref[...].astype(F32) + source(k, part(d, s + 1), d)[...].astype(F32)
-        ref[...] = total.astype(BF)
-
-    def gather(k, d, s):
-        ref = put_at(k, held(d, s), d)
-        return remote(ref, ref, 4 + k, d, s)
-
-    left = n - 1 - AHEAD
-    half = ro_ref.shape[3] // 2
-
-    def ff_hop(kind, c, d, s):
-        ref = (ro_ref, eo_ref)[kind].at[held(d, s), d, :, pl.ds(c * half, half)]
-        k = 2 * kind + c
-        return pltpu.make_async_remote_copy(
-            src_ref=ref,
-            dst_ref=ref,
-            send_sem=fsend.at[k, d],
-            recv_sem=frecv.at[k, d, s - AHEAD],
-            device_id={"dp": sides[d]},
-            device_id_type=MESH_ID,
-        )
-
-    def beside_step(kind, s, act):
-        @pl.when(s < left)
-        def _():
-            for d in range(2):
-                act(ff_hop(kind, 0, d, AHEAD + s))
-
-        @pl.when(s >= n - 1 - left)
-        def _():
-            for d in range(2):
-                act(ff_hop(kind, 1, d, AHEAD + s - (n - 1 - left)))
-
-    def start(copy):
-        copy.start()
-
-    def finish(copy):
-        copy.wait()
-
-    def gather_small(s):
-        ref = sall.at[held(0, s)]
-        return little(ref, ref, 1, s)
-
-    for k, d in streams:
-        remote(source(k, part(d, 0), d), slot(k, 0, d), k, d, 0).start()
-    for k in range(3):
-        share(k).start()
-    branch().start()
-    for k in range(3):
-        share(k).wait()
-    ssum[...] = small_ref[...]
-    shared = n * 6 // 8
-    ssum[0:shared] = ssum[0:shared] + speer[0, 0:shared] + speer[1, 0:shared] + speer[2, 0:shared]
-    little(ssum.at[part(0, 0)], sbuf.at[0], 0, 0).start()
-
-    @pl.loop(0, n - 2)
-    def _(s):
-        beside_step(0, s, start)
-        for k, d in streams:
-            remote(slot(k, s, d), slot(k, s, d), k, d, s).wait()
-            add(k, d, s)
-            remote(slot(k, s, d), slot(k, s + 1, d), k, d, s + 1).start()
-        little(sbuf.at[s], sbuf.at[s], 0, s).wait()
-        sbuf[s] = sbuf[s] + ssum[part(0, s + 1)]
-        little(sbuf.at[s], sbuf.at[s + 1], 0, s + 1).start()
-        beside_step(0, s, finish)
-
-    last = n - 2
-    beside_step(0, last, start)
-    puts = []
-    for k, d in streams:
-        remote(slot(k, last, d), slot(k, last, d), k, d, last).wait()
-        add(k, d, last)
-        put = pltpu.make_async_copy(slot(k, last, d), put_at(k, mine, d), local.at[2 + 2 * k + d])
-        put.start()
-        puts.append(put)
-    for (k, d), put in zip(streams, puts):
-        put.wait()
-        gather(k, d, 0).start()
-    little(sbuf.at[last], sbuf.at[last], 0, last).wait()
-    sall[mine] = sbuf[last] + ssum[mine]
-    gather_small(0).start()
-    beside_step(0, last, finish)
-
-    @pl.loop(0, n - 2)
-    def _(s):
-        beside_step(1, s, start)
-        for k, d in streams:
-            gather(k, d, s).wait()
-            gather(k, d, s + 1).start()
-        gather_small(s).wait()
-        gather_small(s + 1).start()
-        beside_step(1, s, finish)
-
-    beside_step(1, last, start)
-
-    branch().wait()
-    for load in loads:
-        load.wait()
-    step = 64
-
-    @pl.loop(0, bo_ref.shape[0] // step)
-    def _(r):
-        at = pl.ds(pl.multiple_of(r * step, step), step)
-        total = resid[at, :] + brn[at, :].astype(F32) + bro[at, :].astype(F32) + rbias_ref[...]
-        bo_ref[at, :] = total.astype(BF)
-
-    for k, d in streams:
-        gather(k, d, last).wait()
-    gather_small(last).wait()
-    for c in range(n):
-        so_ref[in_row(c)] = sall[c]
-    beside_step(1, last, finish)
-
-
-def ring_sum(g, norm, dsum, usum, qsum, resid, brn, brf, r, e, rbias, n):
-    split = (4, n, 2, g.shape[1] // (2 * n), g.shape[2])
-    s3 = jax.ShapeDtypeStruct((n, 1, 8 * norm.shape[1] // n), F32)
-    small = jax.ShapeDtypeStruct((8, norm.shape[1]), F32)
-    vmem = pl.BlockSpec(memory_space=pltpu.VMEM)
-    anyspace = pl.BlockSpec(memory_space=pl.ANY)
-    qo, mo, ro, eo, so, bo = pl.pallas_call(
-        functools.partial(ring_kernel, n),
-        in_specs=[vmem] * 6 + [anyspace] * 5,
-        out_specs=[anyspace] * 4 + [vmem] * 2,
-        input_output_aliases={9: 2, 10: 3},
-        out_shape=[
-            jax.ShapeDtypeStruct((3,) + split[1:], BF),
-            jax.ShapeDtypeStruct(split[1:], BF),
-            jax.ShapeDtypeStruct(r.shape, BF),
-            jax.ShapeDtypeStruct(e.shape, BF),
-            small,
-            jax.ShapeDtypeStruct(brf.shape, BF),
-        ],
-        scratch_shapes=[
-            pltpu.VMEM((n - 1, 2, 4) + split[3:], BF),
-            pltpu.VMEM(small.shape, F32),
-            pltpu.VMEM(s3.shape, F32),
-            pltpu.VMEM((n - 1,) + s3.shape[1:], F32),
-            pltpu.VMEM(s3.shape, F32),
-            pltpu.VMEM((3,) + s3.shape, F32),
-            pltpu.VMEM(s3.shape, F32),
-            pltpu.VMEM(resid.shape, F32),
-            pltpu.VMEM(brn.shape, BF),
-            pltpu.VMEM(brf.shape, BF),
-            pltpu.SemaphoreType.DMA((8, 2)),
-            pltpu.SemaphoreType.DMA((8, 2, n - 1)),
-            pltpu.SemaphoreType.DMA((4, 2)),
-            pltpu.SemaphoreType.DMA((4, 2, n - 1 - AHEAD)),
-            pltpu.SemaphoreType.DMA((2,)),
-            pltpu.SemaphoreType.DMA((2, n - 1)),
-            pltpu.SemaphoreType.DMA((4,)),
-            pltpu.SemaphoreType.DMA((4,)),
-            pltpu.SemaphoreType.DMA((10,)),
-        ],
-        compiler_params=pltpu.CompilerParams(
-            collective_id=1, has_side_effects=True, vmem_limit_bytes=60 << 20
-        ),
-        name="ring_sum",
-    )(g.reshape(split), norm, dsum, usum, qsum, rbias, resid, brn, brf, r, e)
-    wide = (-1, r.shape[-1])
-    return (
-        qo.reshape((3,) + g.shape[1:]),
-        mo.reshape(g.shape[1:]),
-        ro.reshape(wide),
-        eo.reshape(wide),
-        so,
-        bo,
-    )
 
 
 def finish_kernel(
@@ -1490,7 +1464,7 @@
     resid_grad, mg_all, reduce_grad, expand_grad, br_near, br_far, unit_sums, sums2, carry = ff(
         n2, og_all, w_expand, w_reduce, expand_bias.reshape(1, units), resid, second_gain.reshape(flat), dp_size
     )
-    in_grad, grads, qv_sums, norm_sums, reduce_all, expand_all = backward(
+    in_grad, qkv_grad, mix_grad, reduce_all, expand_all, small, block_out = backward(
         mg_all,
         qkv,
         att,
@@ -1504,21 +1478,13 @@
         reduce_grad,
         expand_grad,
         carry,
-        segments,
-        first_gain.reshape(flat),
-        dp_size,
-    )
-    qkv_grad, mix_grad, reduce_all, expand_all, small, block_out = ring_sum(
-        grads,
-        norm_sums,
-        sums2,
-        unit_sums,
-        qv_sums,
         resid,
         br_near,
         br_far,
-        reduce_all,
-        expand_all,
+        segments,
+        first_gain.reshape(flat),
+        sums2,
+        unit_sums,
         reduce_bias.reshape(flat),
         dp_size,
     )

time: 254 us -> 248 us (0.976)
  Pallas kernels: 252 us -> 247 us
    pallas_call x2 -> x1, Pallas kernels: 138 us -> 132 us  [backward(): pl.pallas_call(functools.partial(bwd_kernel, n), in_specs=[anyspace] * 16...]
where the time goes in v2:
time: 248 us
  Pallas kernels  247 us (100%)
    pallas_call x1, Pallas kernels, backward(): pl.pallas_call(functools.partial(bwd_kernel, n), in_specs=[anyspace] * 16...  132 us
    pallas_call x1, Pallas kernels, ff(): pl.pallas_call(functools.partial(ff_kernel, n), in_specs=[anyspace] * 5 +...  58.1 us
    pallas_call x1, Pallas kernels, forward(): pl.pallas_call(functools.partial(fwd_kernel, n), in_specs=[vmem] * 8 + [a...  47 us
    pallas_call x1, Pallas kernels, finish(): pl.pallas_call(finish_kernel, in_specs=[anyspace] * 6 + [vmem], out_specs...  9.48 us

profile of v2, /device:TPU:0, one launch (start us, length us, event | category | flops | bytes accessed | tf_op | source)
XLA Modules:
  0.0 247.8 jit_solution(12847421833138630553)
XLA Ops:
  0.6 47.0 %forward.1 = (bf16[1024,1024]{1,0:T(8,128)(2,1)}, bf16[1024,1536]{1,0:T(8,128)(2,1)}, bf16[1024,512]{1,0:T(8,128)(2,1)}, f32[512,1024]{1,0:T(8,128)}, bf16[512,1...) custom-call(bf16[512,1024]{1,0:T(8,128)(2,1)} %x_hbm.1, ...), custom_call_target="tpu_custom_call" | custom-call | tf_op jit(solution)/shard_map/forward/pallas_call | solution.py:390
  47.6 58.1 %ff.1 = (f32[512,1024]{1,0:T(8,128)}, bf16[1024,1024]{1,0:T(8,128)(2,1)}, bf16[8,2,64,1024]{3,2,1,0:T(8,128)(2,1)}, bf16[8,2,64,1024]{3,2,1,0:T(8,128)(2,1)}, bf...) custom-call(bf16[512,1024]{1,0:T(8,128)(2,1)} %get-tuple-element.52., ...), custom_call_target="tpu_custom_call" | custom-call | tf_op jit(solution)/shard_map/ff/pallas_call | solution.py:1279
  105.8 132.4 %backward.1 = (f32[512,1024]{1,0:T(8,128)}, bf16[3,8,2,64,256]{4,3,2,1,0:T(8,128)(2,1)}, bf16[8,2,64,256]{3,2,1,0:T(8,128)(2,1)}, bf16[8,2,64,1024]{3,2,1,0:T(8,...) custom-call(bf16[1024,1024]{1,0:T(8,128)(2,1)} %get-tuple-element.55.mg_hbm, ...), custom_call_target="tpu_custom_call" | custom-call | tf_op jit(solution)/shard_map/backward/pallas_call | solution.py:942
  238.1 9.5 %finish.1 = (bf16[512,1024]{1,0:T(8,128)(2,1)}, f32[512,1024]{1,0:T(8,128)}, f32[3,1024,256]{2,1,0:T(8,128)}, f32[256,1024]{1,0:T(8,128)}, f32[1024,1024]{1,0:T(...) custom-call(bf16[3,1024,256]{2,1,0:T(8,128)(2,1)} %bitcast.24, ...), custom_call_target="tpu_custom_call" | custom-call | tf_op jit(solution)/shard_map/finish/pallas_call | solution.py:1394

commit v3 on v2

--- a/solution.py
+++ b/solution.py
@@ -228,7 +228,7 @@
     )
     for load in loads:
         load.start()
-    step = 64
+    step = 128
     for c in range(2):
 
         @pl.loop(0, half // step)
@@ -616,7 +616,7 @@
     branch().wait()
     for load in loads:
         load.wait()
-    step = 64
+    step = 128
 
     @pl.loop(0, bo_ref.shape[0] // step)
     def _(r):
@@ -751,7 +751,7 @@
 
     for kind in range(2):
         for d in range(2):
-            ring_copy(carry_hbm.at[kind, d], kind, d, 1).start()
+            ring_copy(carry_hbm.at[kind, d], kind, d, 2 - kind).start()
 
     fill_bias(seg_ref, me // 2, bias_ref, blocks)
     masks = half_masks()
@@ -813,15 +813,15 @@
             off += keys
             late = 2 * pairs + blocks * (q - pairs) + i
 
-            @pl.when(jnp.logical_and(q >= pairs, late < 2 * (n - 2)))
+            @pl.when(jnp.logical_and(q >= pairs, late < 2 * (n - 2) - 1))
             def _():
-                tick(i % 2, 1 + late // 2)
+                tick(1 - i % 2, 1 + i % 2 + late // 2)
 
             if i % 2 == 1:
 
                 @pl.when(first)
                 def _():
-                    tick(i // 2, 1 + q)
+                    tick(1 - i // 2, 1 + i // 2 + q)
 
         dv = dv_ref[...].astype(BF)
         dqkv[:, lanes(1)] = dk_ref[...].astype(BF)
@@ -846,10 +846,13 @@
                 q_send[k] = dot(rows1[...], dqkv[:, to], TN).astype(BF)
                 q_across(k).start()
 
-    @pl.loop(1 + turns // 2, n - 1)
-    def _(s):
-        for kind in range(2):
-            tick(kind, s)
+    if n - 2 > turns // 2:
+        tick(1, 1 + turns // 2)
+
+        @pl.loop(2 + turns // 2, n - 1)
+        def _(s):
+            for kind in range(2):
+                tick(kind, s)
 
     gather_begin()
     for k in (8, 9):
@@ -882,7 +885,7 @@
     load(10).wait()
     load(11).wait()
     nsum_ref[...] = jnp.zeros_like(nsum_ref)
-    step = 64
+    step = 128
 
     @pl.loop(0, rows // step)
     def _(r):
@@ -1034,7 +1037,7 @@
     rgrad_out, mg_out, rg_out, eg_out, brn_out, brf_out, usum_ref, dsum_ref, carry_ref,
     rgrad_ref, mg_ref, rg_ref, eg_ref, brn_ref, brf_ref,
     og_ref, we_ref, wr_ref, resid_ref, n2b, act, pg, ng, br, ng_d, br_d, ng_s, br_s, ng_far, ng_out,
-    rbuf, send, recv, ring_send, ring_recv, local, out,
+    rbuf, rbuf2, send, recv, ring_send, ring_recv, local, out,
 ):
     rows, width = n2_ref.shape
     units = we_ref.shape[1]
@@ -1200,6 +1203,16 @@
             device_id_type=MESH_ID,
         )
 
+    def second_hop(d):
+        return pltpu.make_async_remote_copy(
+            src_ref=rbuf.at[0, d],
+            dst_ref=rbuf2.at[d],
+            send_sem=ring_send.at[2, d],
+            recv_sem=ring_recv.at[2, d],
+            device_id={"dp": sides[d]},
+            device_id_type=MESH_ID,
+        )
+
     @pl.loop(0, width // nb)
     def _(k):
         cols = pl.ds(pl.multiple_of(k * nb, nb), nb)
@@ -1231,7 +1244,7 @@
     ng_beside().wait()
     loads[5].wait()
     dsum_ref[...] = jnp.zeros_like(dsum_ref)
-    step = 64
+    step = 128
     for c in range(2):
         ng_across(c).wait()
 
@@ -1258,12 +1271,21 @@
         mg_beside(c).start()
         put(4 + c).start()
         put(6 + c).start()
-
-    for kind in range(2):
-        for d in range(2):
-            ring_copy(kind, d).wait()
-            total = rbuf[kind, d].astype(F32) + ffg[kind][part_of(d, 1), d].astype(F32)
-            carry_ref[kind, d] = total.astype(BF)
+        if c == 0:
+            for d in range(2):
+                ring_copy(0, d).wait()
+                total = rbuf[0, d].astype(F32) + rg_ref[part_of(d, 1), d].astype(F32)
+                rbuf[0, d] = total.astype(BF)
+                second_hop(d).start()
+
+    for d in range(2):
+        second_hop(d).wait()
+        total = rbuf2[d].astype(F32) + rg_ref[part_of(d, 2), d].astype(F32)
+        carry_ref[0, d] = total.astype(BF)
+    for d in range(2):
+        ring_copy(1, d).wait()
+        total = rbuf[1, d].astype(F32) + eg_ref[part_of(d, 1), d].astype(F32)
+        carry_ref[1, d] = total.astype(BF)
     for c in range(2):
         mg_beside(c).wait()
     for k in range(8):
@@ -1314,10 +1336,11 @@
             pltpu.VMEM((2, part, width), BF),
             pltpu.VMEM((2, part, width), BF),
             pltpu.VMEM((2, 2, units // (2 * n), width), BF),
+            pltpu.VMEM((2, units // (2 * n), width), BF),
             pltpu.SemaphoreType.DMA((15,)),
             pltpu.SemaphoreType.DMA((15,)),
-            pltpu.SemaphoreType.DMA((2, 2)),
-            pltpu.SemaphoreType.DMA((2, 2)),
+            pltpu.SemaphoreType.DMA((3, 2)),
+            pltpu.SemaphoreType.DMA((3, 2)),
             pltpu.SemaphoreType.DMA((6,)),
             pltpu.SemaphoreType.DMA((8,)),
         ],
@@ -1370,7 +1393,7 @@
     puts[0].start()
     for k, (_src, mid, wide, dst) in enumerate(jobs):
         gets[k].wait()
-        step = 64
+        step = 128
 
         @pl.loop(0, mid.shape[0] // step)
         def _(r):

time: 248 us -> 247 us (level)
  no operation moved by 1% of the time
where the time goes in v3:
time: 247 us
  Pallas kernels  246 us (100%)
    pallas_call x1, Pallas kernels, backward(): pl.pallas_call(functools.partial(bwd_kernel, n), in_specs=[anyspace] * 16...  131 us
    pallas_call x1, Pallas kernels, ff(): pl.pallas_call(functools.partial(ff_kernel, n), in_specs=[anyspace] * 5 +...  59.5 us
    pallas_call x1, Pallas kernels, forward(): pl.pallas_call(functools.partial(fwd_kernel, n), in_specs=[vmem] * 8 + [a...  46.3 us
    pallas_call x1, Pallas kernels, finish(): pl.pallas_call(finish_kernel, in_specs=[anyspace] * 6 + [vmem], out_specs...  9.48 us

profile of v3, /device:TPU:0, one launch (start us, length us, event | category | flops | bytes accessed | tf_op | source)
XLA Modules:
  0.0 246.9 jit_solution(2408890322106902075)
XLA Ops:
  0.6 46.3 %forward.1 = (bf16[1024,1024]{1,0:T(8,128)(2,1)}, bf16[1024,1536]{1,0:T(8,128)(2,1)}, bf16[1024,512]{1,0:T(8,128)(2,1)}, f32[512,1024]{1,0:T(8,128)}, bf16[512,1...) custom-call(bf16[512,1024]{1,0:T(8,128)(2,1)} %x_hbm.1, ...), custom_call_target="tpu_custom_call" | custom-call | tf_op jit(solution)/shard_map/forward/pallas_call | solution.py:390
  46.9 59.5 %ff.1 = (f32[512,1024]{1,0:T(8,128)}, bf16[1024,1024]{1,0:T(8,128)(2,1)}, bf16[8,2,64,1024]{3,2,1,0:T(8,128)(2,1)}, bf16[8,2,64,1024]{3,2,1,0:T(8,128)(2,1)}, bf...) custom-call(bf16[512,1024]{1,0:T(8,128)(2,1)} %get-tuple-element.52., ...), custom_call_target="tpu_custom_call" | custom-call | tf_op jit(solution)/shard_map/ff/pallas_call | solution.py:1301
  106.4 130.8 %backward.1 = (f32[512,1024]{1,0:T(8,128)}, bf16[3,8,2,64,256]{4,3,2,1,0:T(8,128)(2,1)}, bf16[8,2,64,256]{3,2,1,0:T(8,128)(2,1)}, bf16[8,2,64,1024]{3,2,1,0:T(8,...) custom-call(bf16[1024,1024]{1,0:T(8,128)(2,1)} %get-tuple-element.55.mg_hbm, ...), custom_call_target="tpu_custom_call" | custom-call | tf_op jit(solution)/shard_map/backward/pallas_call | solution.py:945
  237.3 9.5 %finish.1 = (bf16[512,1024]{1,0:T(8,128)(2,1)}, f32[512,1024]{1,0:T(8,128)}, f32[3,1024,256]{2,1,0:T(8,128)}, f32[256,1024]{1,0:T(8,128)}, f32[1024,1024]{1,0:T(...) custom-call(bf16[3,1024,256]{2,1,0:T(8,128)(2,1)} %bitcast.24, ...), custom_call_target="tpu_custom_call" | custom-call | tf_op jit(solution)/shard_map/finish/pallas_call | solution.py:1417
